TPU v7x, 128 devices: a whole 4x4x4 slice. The times are simulated.
128 devices in a mesh: grp: 16 (over x, y), mem: 8 (over z, core).
Axes of the slice: x: 4, y: 4, z: 4, core: 2. Of those that a mesh axis runs over, the one named last changes fastest.
Arguments:
- filterbank: float32 [16, 8, 8, 16000], P('grp', 'mem'), may hold values from -6 to 6
- destination: int32 [16, 64], P('grp', 'mem'), may hold values from 0 to 15, as said below
- initial_conv_weight: bfloat16 [400, 1024], replicated, may hold values from -0.3125 to 0.3125
- expand_weight: bfloat16 [1024, 1024], replicated, may hold values from -0.1875 to 0.1875
- branch_weight: bfloat16 [7, 384, 128], replicated, may hold values from -0.3125 to 0.3125
- merge_weight: bfloat16 [1024, 1024], replicated, may hold values from -0.1875 to 0.1875
- squeeze_weight: bfloat16 [1024, 128], replicated, may hold values from -0.1875 to 0.1875
- excite_weight: bfloat16 [128, 1024], replicated, may hold values from -0.5 to 0.5
- attend_weight: bfloat16 [16, 3072, 128], P('grp'), may hold values from -0.1875 to 0.1875
- score_weight: bfloat16 [16, 128, 1024], P('grp'), may hold values from -0.5 to 0.5
- embed_weight: bfloat16 [16, 2048, 192], P('grp'), may hold values from -0.125 to 0.125
- language_weight: bfloat16 [16, 192, 107], P('grp'), may hold values from -0.4375 to 0.4375
Outputs:
- language_logits: float32 [16, 64, 107], P('grp', 'mem')
- similarity: float32 [16, 64, 64], P('grp', 'mem')
Inputs may be any that keep to these rules, and one draw needn't show every extreme that they name: `destination`: each device sends its 8 segments to 8 different groups, so at most 1 to any group. For every index of mem, one group receives exactly 16 segments from the devices of that index, and no group receives more.
All inputs are finite; a program needn't handle non-finite values.
Results may differ from a plain program's by a relative error of at most 0.0075.
Values may be sent and summed in bfloat16 or wider, within the bound.
No kernel may reach another device: no remote copies, remote signals or barrier semaphores. Data moves between devices by JAX's collectives and lax.ppermute only.
A program may use at most 128 MiB of HBM per device.

v0:
```python
import functools

import jax
import jax.numpy as jnp
from jax import lax
from jax.experimental import pallas as pl
from jax.experimental.pallas import tpu as pltpu
from jax.sharding import PartitionSpec as P

MELS = 80
CH = 1024
BR = 128
SCALE = 8
ATT = 128
EMB = 192
LANGS = 107
FRAMES = 200
STORE = 8
SLOTS = 16
LANES = 128

FLAT = FRAMES * MELS // LANES
ROWS = 128

SUPER = 8
NSUPER = FRAMES // SUPER
WIDE = SUPER * MELS
BLOCKS = WIDE // LANES
TAPS = 5 * MELS
PAD_TOP = 112

EPS_STAT = 1e-05
EPS_NORM = 1e-06

F32 = jnp.float32
BF16 = jnp.bfloat16


def dot(a, b):
    return jnp.dot(a, b, preferred_element_type=F32)


def exact_dot(a, b):
    rows = a.shape[0]
    high = a.astype(BF16)
    rest = a - high.astype(F32)
    mid = rest.astype(BF16)
    low = (rest - mid.astype(F32)).astype(BF16)
    out = dot(jnp.concatenate([high, mid, low], axis=0), b)
    return out[:rows] + (out[rows : 2 * rows] + out[2 * rows :])


def pack_kernel(dest_ref, bank_ref, out_ref, row_ref):
    out_ref[...] = jnp.zeros_like(out_ref)
    for s in range(STORE):
        row_ref[:FLAT] = bank_ref[:, s, :]
        row_ref[FLAT:] = jnp.full((ROWS - FLAT, LANES), s + 1, F32)
        out_ref[dest_ref[s]] = row_ref[...].astype(BF16)


def pack(bank, dest):
    return pl.pallas_call(
        pack_kernel,
        out_shape=jax.ShapeDtypeStruct((SLOTS, ROWS, LANES), BF16),
        in_specs=[
            pl.BlockSpec(memory_space=pltpu.SMEM),
            pl.BlockSpec(memory_space=pltpu.VMEM),
        ],
        out_specs=pl.BlockSpec(memory_space=pltpu.VMEM),
        scratch_shapes=[pltpu.VMEM((ROWS, LANES), F32)],
        name="pack",
    )(dest, bank)


def family_kernel(
    recv_ref,
    front_w,
    expand_w,
    pair_w,
    merge_w,
    squeeze_w,
    excite_w,
    attend_w,
    score_w,
    embed_w,
    lang_w,
    out_ref,
    flat,
    bank,
    front,
    wide,
    joined,
    merged,
    pre,
    attended,
    total,
    first,
    second,
    third,
):
    mb = 20
    for s in range(SLOTS):
        flat[:, s, :] = recv_ref[s].astype(F32)
    header = flat[FLAT]
    bank[0] = jnp.zeros((SLOTS, WIDE), BF16)
    bank[NSUPER + 1] = jnp.zeros((SLOTS, WIDE), BF16)
    for r in range(NSUPER):
        bank[r + 1] = jnp.concatenate(
            [flat[BLOCKS * r + t].astype(BF16) for t in range(BLOCKS)], axis=1
        )

    def front_cols(n, carry):
        cols = pl.ds(pl.multiple_of(n * 256, 256), 256)
        for j in range(SUPER):
            start = MELS * (j - 2)
            block, offset = start // LANES, start % LANES
            pieces = []
            for t in range(block, block + 4):
                shift, lane = t // BLOCKS, t % BLOCKS
                pieces.append(
                    bank[1 + shift : 1 + shift + NSUPER, :, lane * LANES : (lane + 1) * LANES]
                )
            window = jnp.concatenate(pieces, axis=2).reshape(NSUPER * SLOTS, 4 * LANES)
            top = PAD_TOP - offset
            out = dot(window, front_w[top : top + 4 * LANES, cols])
            front[:, j, :, cols] = (
                jnp.maximum(out, 0.0).astype(BF16).reshape(NSUPER, SLOTS, 256)
            )
        return carry

    lax.fori_loop(0, CH // 256, front_cols, 0)

    frames = front.reshape(FRAMES, SLOTS, CH)

    edge = jnp.zeros((2, SLOTS, CH), BF16)
    wide[0:2] = edge
    wide[FRAMES + 2 : FRAMES + 4] = edge

    def expand_rows(c, carry):
        f0 = c * mb
        rows = frames[pl.ds(f0, mb)].reshape(mb * SLOTS, CH)
        for n in range(CH // 256):
            cols = slice(n * 256, (n + 1) * 256)
            out = jnp.maximum(dot(rows, expand_w[:, cols]), 0.0).astype(BF16)
            out = out.reshape(mb, SLOTS, 256)
            wide[pl.ds(f0 + 2, mb), :, cols] = out
            if n == 0:
                joined[pl.ds(f0, mb), :, :BR] = out[:, :, :BR]
        return carry

    lax.fori_loop(0, FRAMES // mb, expand_rows, 0)

    quads = wide.reshape(FRAMES // 4 + 1, 4, SLOTS, CH)
    outs = joined.reshape(FRAMES // 4, 4, SLOTS, CH)
    bc = FRAMES // 8

    def branch(i, last):
        cols = pl.ds(pl.multiple_of(i * BR, BR), BR)
        after = pl.ds(pl.multiple_of((i + 1) * BR, BR), BR)
        weight = pair_w[i - 1]
        for half in range(2):
            for p in range(2):
                b0 = half * bc
                rows = jnp.concatenate(
                    [
                        quads[b0 : b0 + bc, p, :, cols],
                        quads[b0 : b0 + bc, p + 2, :, cols],
                        quads[b0 + 1 : b0 + 1 + bc, p, :, cols],
                        quads[b0 + 1 : b0 + 1 + bc, p + 2, :, cols],
                    ],
                    axis=2,
                ).reshape(bc * SLOTS, 4 * BR)
                out = jnp.maximum(dot(rows, weight), 0.0).astype(BF16)
                out = out.reshape(bc, SLOTS, 2 * BR)
                early, late = out[:, :, :BR], out[:, :, BR:]
                outs[b0 : b0 + bc, p, :, cols] = early
                outs[b0 : b0 + bc, p + 2, :, cols] = late
                if not last:
                    at = quads[b0 : b0 + bc, p + 2, :, after]
                    quads[b0 : b0 + bc, p + 2, :, after] = at + early
                    at = quads[b0 + 1 : b0 + 1 + bc, p, :, after]
                    quads[b0 + 1 : b0 + 1 + bc, p, :, after] = at + late

    def branch_step(i, carry):
        branch(i, False)
        return carry

    lax.fori_loop(1, SCALE - 1, branch_step, 0)
    branch(SCALE - 1, True)

    total[...] = jnp.zeros_like(total)

    def merge_rows(c, carry):
        f0 = c * mb
        rows = joined[pl.ds(f0, mb)].reshape(mb * SLOTS, CH)
        for n in range(CH // 256):
            cols = slice(n * 256, (n + 1) * 256)
            out = jnp.maximum(dot(rows, merge_w[:, cols]), 0.0).reshape(mb, SLOTS, 256)
            merged[pl.ds(f0, mb), :, cols] = out
            total[:, cols] += jnp.sum(out, axis=0)
        return carry

    lax.fori_loop(0, FRAMES // mb, merge_rows, 0)

    squeezed = total[...] * (1.0 / FRAMES)
    hidden = jnp.maximum(exact_dot(squeezed, squeeze_w[...]), 0.0)
    total[...] = jax.nn.sigmoid(exact_dot(hidden, excite_w[...]))

    first[...] = jnp.zeros_like(first)
    second[...] = jnp.zeros_like(second)
    third[...] = (
        (frames[0].astype(F32) + merged[0] * total[...]).astype(BF16).astype(F32)
    )

    def trunk_rows(c, carry):
        f0 = c * mb
        acc = jnp.zeros((mb * SLOTS, ATT), F32)
        for n in range(CH // 256):
            cols = slice(n * 256, (n + 1) * 256)
            out = (
                frames[pl.ds(f0, mb), :, cols].astype(F32)
                + merged[pl.ds(f0, mb), :, cols] * total[:, cols][None]
            ).astype(BF16)
            frames[pl.ds(f0, mb), :, cols] = out
            off = out.astype(F32) - third[:, cols][None]
            first[:, cols] += jnp.sum(off, axis=0)
            second[:, cols] += jnp.sum(off * off, axis=0)
            acc = acc + dot(out.reshape(mb * SLOTS, 256), attend_w[cols, :])
        pre[pl.ds(f0, mb)] = acc.reshape(mb, SLOTS, ATT)
        return carry

    lax.fori_loop(0, FRAMES // mb, trunk_rows, 0)

    drift = first[...] * (1.0 / FRAMES)
    center = third[...] + drift
    variance = jnp.maximum(second[...] * (1.0 / FRAMES) - drift * drift, 0.0)
    spread = jnp.sqrt(variance + EPS_STAT)
    context = exact_dot(center, attend_w[CH : 2 * CH]) + exact_dot(spread, attend_w[2 * CH :])
    attended[...] = jnp.tanh(pre[...] + context[None]).astype(BF16)

    third[...] = center
    total[...] = 1.0 / spread
    pooled_mean, pooled_dev = [], []
    for n in range(CH // 256):
        cols = slice(n * 256, (n + 1) * 256)
        shift = third[:, cols]
        scale = total[:, cols]

        def pool_rows(c, carry, cols=cols, shift=shift, scale=scale):
            s0, s1, s2 = carry
            f0 = c * mb
            rows = attended[pl.ds(f0, mb)].reshape(mb * SLOTS, ATT)
            energy = dot(rows, score_w[:, cols]).reshape(mb, SLOTS, 256)
            weight = jnp.exp(energy)
            z = (frames[pl.ds(f0, mb), :, cols].astype(F32) - shift[None]) * scale[None]
            wz = weight * z
            s0 = s0 + jnp.sum(weight, axis=0)
            s1 = s1 + jnp.sum(wz, axis=0)
            s2 = s2 + jnp.sum(wz * z, axis=0)
            return s0, s1, s2

        zero = jnp.zeros((SLOTS, 256), F32)
        s0, s1, s2 = lax.fori_loop(0, FRAMES // mb, pool_rows, (zero, zero, zero))
        m1 = s1 / s0
        m2 = jnp.maximum(s2 / s0 - m1 * m1, 0.0)
        dev = 1.0 / scale
        pooled_mean.append(shift + m1 * dev)
        pooled_dev.append(jnp.sqrt(m2 * dev * dev + EPS_STAT))
    pooled = jnp.concatenate(pooled_mean + pooled_dev, axis=1).astype(BF16)
    embedding = dot(pooled, embed_w[...])
    logits = dot(embedding.astype(BF16), lang_w[...])
    mean_square = jnp.mean(jnp.square(embedding), axis=1, keepdims=True)
    normed = (embedding * lax.rsqrt(mean_square + EPS_NORM)).astype(BF16).astype(F32)
    parts = [
        normed[:, :LANES],
        jnp.concatenate([normed[:, LANES:], jnp.zeros((SLOTS, 2 * LANES - EMB), F32)], axis=1),
        jnp.concatenate([logits, jnp.zeros((SLOTS, LANES - LANGS), F32)], axis=1),
        header,
    ]
    for k, part in enumerate(parts):
        for m in range(8):
            out_ref[:, m, k, :] = part


def family(recv, weights):
    vmem = pl.BlockSpec(memory_space=pltpu.VMEM)
    return pl.pallas_call(
        family_kernel,
        out_shape=jax.ShapeDtypeStruct((SLOTS, 8, 4, LANES), F32),
        in_specs=[vmem] * (1 + len(weights)),
        out_specs=vmem,
        scratch_shapes=[
            pltpu.VMEM((ROWS, SLOTS, LANES), F32),
            pltpu.VMEM((NSUPER + 2, SLOTS, WIDE), BF16),
            pltpu.VMEM((NSUPER, SUPER, SLOTS, CH), BF16),
            pltpu.VMEM((FRAMES + 4, SLOTS, CH), BF16),
            pltpu.VMEM((FRAMES, SLOTS, CH), BF16),
            pltpu.VMEM((FRAMES, SLOTS, CH), F32),
            pltpu.VMEM((FRAMES, SLOTS, ATT), F32),
            pltpu.VMEM((FRAMES, SLOTS, ATT), BF16),
            pltpu.VMEM((SLOTS, CH), F32),
            pltpu.VMEM((SLOTS, CH), F32),
            pltpu.VMEM((SLOTS, CH), F32),
            pltpu.VMEM((SLOTS, CH), F32),
        ],
        compiler_params=pltpu.CompilerParams(vmem_limit_bytes=58 << 20),
        cost_estimate=pl.CostEstimate(
            flops=20_000_000_000, bytes_accessed=10_000_000, transcendentals=4_000_000
        ),
        name="family",
    )(recv, *weights)


def home_kernel(mem_ref, recv_ref, logits_ref, sim_ref, held):
    head0, head1 = recv_ref[:, 0, :], recv_ref[:, 1, :]
    mark = recv_ref[:, 3, :]
    rows = recv_ref.shape[0]
    row = lax.broadcasted_iota(jnp.int32, (rows, LANES), 0)
    lane = lax.broadcasted_iota(jnp.int32, (rows, LANES), 1)
    place = lax.rem(row, 8) * STORE + mark.astype(jnp.int32) - 1
    pick = jnp.where((mark > 0.5) & (place == lane), 1.0, 0.0)
    pick16 = pick.astype(BF16)
    turned = (((0,), (0,)), ((), ()))
    normed = lax.dot_general(
        pick16,
        jnp.concatenate([head0, head1], axis=1).astype(BF16),
        turned,
        preferred_element_type=F32,
    )
    held[:, : 2 * LANES] = normed
    held[:, 2 * LANES :] = lax.dot_general(
        pick, recv_ref[:, 2, :], turned, preferred_element_type=F32, precision=lax.Precision.HIGHEST
    )
    own = held[pl.ds(pl.multiple_of(mem_ref[0] * STORE, STORE), STORE)]
    logits_ref[0] = own[:, 2 * LANES : 2 * LANES + LANGS]
    sim = lax.dot_general(
        own[:, : 2 * LANES].astype(BF16),
        normed[: 8 * STORE].astype(BF16),
        (((1,), (1,)), ((), ())),
        preferred_element_type=F32,
    )
    sim_ref[0] = sim / EMB


def home(member, recv):
    vmem = pl.BlockSpec(memory_space=pltpu.VMEM)
    return pl.pallas_call(
        home_kernel,
        out_shape=(
            jax.ShapeDtypeStruct((1, STORE, LANGS), F32),
            jax.ShapeDtypeStruct((1, STORE, 8 * STORE), F32),
        ),
        in_specs=[pl.BlockSpec(memory_space=pltpu.SMEM), vmem],
        out_specs=(vmem, vmem),
        scratch_shapes=[pltpu.VMEM((LANES, 3 * LANES), F32)],
        name="home",
    )(member, recv)


def prepare(initial_conv_weight, branch_weight):
    tall = jnp.pad(initial_conv_weight, ((PAD_TOP, PAD_TOP), (0, 0)))
    early = jnp.pad(branch_weight, ((0, 0), (0, BR), (0, 0)))
    late = jnp.pad(branch_weight, ((0, 0), (BR, 0), (0, 0)))
    return tall, jnp.concatenate([early, late], axis=2)


def shards(
    filterbank,
    destination,
    initial_conv_weight,
    expand_weight,
    branch_weight,
    merge_weight,
    squeeze_weight,
    excite_weight,
    attend_weight,
    score_weight,
    embed_weight,
    language_weight,
):
    bank = filterbank.reshape(STORE, FLAT, LANES).transpose(1, 0, 2)
    outbound = pack(bank, destination.reshape(STORE))
    arrived = lax.all_to_all(outbound, "grp", split_axis=0, concat_axis=0, tiled=True)
    tall, pairs = prepare(initial_conv_weight, branch_weight)
    scored = family(
        arrived,
        (
            tall,
            expand_weight,
            pairs,
            merge_weight,
            squeeze_weight,
            excite_weight,
            attend_weight[0],
            score_weight[0],
            embed_weight[0],
            language_weight[0],
        ),
    )
    back = lax.all_to_all(
        scored.reshape(SLOTS * 8, 4, LANES),
        ("grp", "mem"),
        split_axis=0,
        concat_axis=0,
        tiled=True,
    )
    member = lax.axis_index("mem").astype(jnp.int32).reshape(1)
    return home(member, back)


def solution(mesh):
    return jax.shard_map(
        shards,
        mesh=mesh,
        in_specs=(
            P("grp", "mem", None, None),
            P("grp", "mem"),
            P(),
            P(),
            P(),
            P(),
            P(),
            P(),
            P("grp", None, None),
            P("grp", None, None),
            P("grp", None, None),
            P("grp", None, None),
        ),
        out_specs=(P("grp", "mem", None), P("grp", "mem", None)),
        check_vma=False,
    )
```

profile of v0, /device:TPU:1, one launch (start us, length us, event | category | flops | bytes accessed | tf_op | source)
XLA Modules:
  0.0 96.1 jit_solution(3738337869826285314)
XLA Ops:
  0.6 0.0 copy-start.2
  0.6 0.0 copy-start.1
  0.7 2.3 %pack.1 = bf16[16,128,128]{2,1,0:T(8,128)(2,1)} custom-call(s32[8]{0:T(128)} %bitcast.13, f32[125,8,128]{2,1,0:T(8,128)} %bitcast.11), custom_call_target="tpu_custom_call" | custom-call | tf_op jit(solution)/shard_map/pack/pallas_call | solution.py:62
  3.0 7.6 %all-to-all-start = ((bf16[16,128,128]{2,1,0:T(8,128)(2,1)}), bf16[16,128,128]{2,1,0:T(8,128)(2,1)S(1)}, u32[]{:S(2)}, u32[]{:S(2)}) async-start(bf16[16,128,128]{2,1,0:T(8,128)(2,1)} %pack.1), calls=%async_computation | async-start | bytes 1048576 | tf_op jit(solution)/shard_map/all_to_all | solution.py:383
  10.5 0.0 copy-done.2
  10.6 0.0 copy-start.3
  10.6 1.3 %copy.14 = bf16[1,2048,192]{2,1,0:T(8,128)(2,1)} copy(bf16[1,2048,192]{1,2,0:T(8,128)(2,1)S(1)} %copy-done.2) | data formatting | bytes 1572864 | tf_op args[10]
  11.9 0.0 copy-done.1
  11.9 1.2 %pad.12.front_w = bf16[624,1024]{1,0:T(8,128)(2,1)} pad(bf16[400,1024]{1,0:T(8,128)(2,1)S(1)} %copy-done.1, bf16[]{:T(256)} %constant.6.clone.1), padding=112_112x0_0 | pad | bytes 2097154 | tf_op jit(solution)/shard_map/jit(_pad)/pad | solution.py:361
  13.1 0.0 copy-done.3
  13.1 1.4 %fusion.2.pair_w = bf16[7,512,256]{2,1,0:T(8,128)(2,1)} fusion(bf16[7,384,128]{2,1,0:T(8,128)(2,1)S(1)} %copy-done.3), kind=kLoop, calls=%fused_computation.4 | loop fusion | flops 7340032 | bytes 2523136 | tf_op jit(solution)/shard_map/concatenate | solution.py:364
  14.6 6.3 %all-to-all-done.recv_ref = bf16[16,128,128]{2,1,0:T(8,128)(2,1)S(1)} async-done(((bf16[16,128,128]{2,1,0:T(8,128)(2,1)}), bf16[16,128,128]{2,1,0:T(8,128)(2,1)S(1)}, u32[]{:S(2)}, u32[]{:S(2)}) %all-to-all-start) | async-done | bytes 524320 | tf_op jit(solution)/shard_map/all_to_all | solution.py:383
  20.8 0.0 copy-start.4
  20.9 0.8 copy-done.4
  21.7 52.1 %family.1 = f32[16,8,4,128]{3,2,1,0:T(4,128)} custom-call(bf16[16,128,128]{2,1,0:T(8,128)(2,1)} %copy-done.4, bf16[624,1024]{1,0:T(8,128)(2,1)} %pad.12.front_w, bf16[1024,1024]{1,0:T(8,128)(2,1)} %expand_w.1, bf16[7,512,256]{2,1,0:T(8,128)(2,1)} %fusion.2.pair_w, bf16[1024,1024]{1,0:T(8,128)(2,1)} %merge_w.1, bf16[1024,128]{1,0:T(8,128)(2,1)} %squeeze_w.1, ...), custom_call_target="tpu_custom_call" | custom-call | flops 20000000000 | bytes 10000000 | tf_op jit(solution)/shard_map/family/pallas_call | solution.py:287
  73.7 8.6 %all-to-all-start.1 = ((f32[128,4,128]{2,1,0:T(4,128)}), f32[128,4,128]{2,1,0:T(4,128)S(1)}, u32[]{:S(2)}, u32[]{:S(2)}) async-start(f32[128,4,128]{2,1,0:T(4,128)} %bitcast.12), calls=%async_computation.1 | async-start | bytes 524288 | tf_op jit(solution)/shard_map/all_to_all | solution.py:400
  82.3 10.9 %all-to-all-done.1.recv_ref = f32[128,4,128]{2,1,0:T(4,128)S(1)} async-done(((f32[128,4,128]{2,1,0:T(4,128)}), f32[128,4,128]{2,1,0:T(4,128)S(1)}, u32[]{:S(2)}, u32[]{:S(2)}) %all-to-all-start.1) | async-done | bytes 262176 | tf_op jit(solution)/shard_map/all_to_all | solution.py:400
  93.2 0.0 copy-start
  93.2 0.7 copy-done
  93.9 2.2 %home.1 = (f32[1,8,107]{2,1,0:T(8,128)}, f32[1,8,64]{2,1,0:T(8,128)}) custom-call(s32[1]{0:T(128)} %bitcast.mem_ref, f32[128,4,128]{2,1,0:T(4,128)} %copy-done), custom_call_target="tpu_custom_call" | custom-call | tf_op jit(solution)/shard_map/home/pallas_call | solution.py:347
Async XLA Ops:
  0.6 9.9 %copy-start.2 = (bf16[1,2048,192]{1,2,0:T(8,128)(2,1)S(1)}, bf16[1,2048,192]{1,2,0:T(8,128)(2,1)}, u32[]{:S(2)}) copy-start(bf16[1,2048,192]{1,2,0:T(8,128)(2,1)} %param.22) | copy-start | bytes 2359300
  0.6 11.2 %copy-start.1 = (bf16[400,1024]{1,0:T(8,128)(2,1)S(1)}, bf16[400,1024]{1,0:T(8,128)(2,1)}, u32[]{:S(2)}) copy-start(bf16[400,1024]{1,0:T(8,128)(2,1)} %param.14) | copy-start | bytes 2457604
  3.0 17.9 %all-to-all-start = ((bf16[16,128,128]{2,1,0:T(8,128)(2,1)}), bf16[16,128,128]{2,1,0:T(8,128)(2,1)S(1)}, u32[]{:S(2)}, u32[]{:S(2)}) async-start(bf16[16,128,128]{2,1,0:T(8,128)(2,1)} %pack.1), calls=%async_computation | async-start | bytes 1048576 | tf_op jit(solution)/shard_map/all_to_all | solution.py:383
  10.6 2.5 %copy-start.3 = (bf16[7,384,128]{2,1,0:T(8,128)(2,1)S(1)}, bf16[7,384,128]{2,1,0:T(8,128)(2,1)}, u32[]{:S(2)}) copy-start(bf16[7,384,128]{2,1,0:T(8,128)(2,1)} %param.16) | copy-start | bytes 2064388
  20.8 0.8 copy-start.4
  73.7 19.5 %all-to-all-start.1 = ((f32[128,4,128]{2,1,0:T(4,128)}), f32[128,4,128]{2,1,0:T(4,128)S(1)}, u32[]{:S(2)}, u32[]{:S(2)}) async-start(f32[128,4,128]{2,1,0:T(4,128)} %bitcast.12), calls=%async_computation.1 | async-start | bytes 524288 | tf_op jit(solution)/shard_map/all_to_all | solution.py:400
  93.2 0.7 copy-start
where the time goes:
time: 96.4 us; the launch traced here: 96.1 us
  Pallas kernels  56.5 us (59%)
  waiting for transfers between devices  17.2 us (18%)
  starting transfers between devices  16.2 us (17%)
  local copies, waits for them, and re-layouts  4.04 us (4%)
  other arithmetic  1.45 us (2%)
    pallas_call x1, Pallas kernels, family(): pl.pallas_call(family_kernel, out_shape=jax.ShapeDtypeStruct((SLOTS, 8, 4...  52.1 us
    all_to_all x1, waiting for transfers between devices, shards(): lax.all_to_all(scored.reshape(SLOTS * 8, 4, LANES), ('grp', 'mem'), split...  10.9 us
    all_to_all x1, starting transfers between devices, shards(): lax.all_to_all(scored.reshape(SLOTS * 8, 4, LANES), ('grp', 'mem'), split...  8.58 us
    all_to_all x1, starting transfers between devices, shards(): lax.all_to_all(outbound, 'grp', split_axis=0, concat_axis=0, tiled=True)  7.58 us
    all_to_all x1, waiting for transfers between devices, shards(): lax.all_to_all(outbound, 'grp', split_axis=0, concat_axis=0, tiled=True)  6.3 us
    unnamed x11, local copies, waits for them, and re-layouts  2.81 us
    pallas_call x1, Pallas kernels, pack(): pl.pallas_call(pack_kernel, out_shape=jax.ShapeDtypeStruct((SLOTS, ROWS,...  2.3 us
    pallas_call x1, Pallas kernels, home(): pl.pallas_call(home_kernel, out_shape=(jax.ShapeDtypeStruct((1, STORE, LA...  2.19 us
  transfers between devices with their start and end apart: 2, of which 2 were waited for; matrix products, arithmetic and copies ran while one was open for 4% of the time, Pallas kernels for 0%

commit v1 on v0

v1 whole, which is shorter than its diff:
```python
import functools

import jax
import jax.numpy as jnp
from jax import lax
from jax.experimental import pallas as pl
from jax.experimental.pallas import tpu as pltpu
from jax.sharding import PartitionSpec as P

MELS = 80
CH = 1024
BR = 128
SCALE = 8
ATT = 128
EMB = 192
LANGS = 107
FRAMES = 200
STORE = 8
SLOTS = 16
LANES = 128

FLAT = FRAMES * MELS // LANES
ROWS = 128

SUPER = 8
NSUPER = FRAMES // SUPER
WIDE = SUPER * MELS
BLOCKS = WIDE // LANES
TAPS = 5 * MELS
PAD_TOP = 112

EPS_STAT = 1e-05
EPS_NORM = 1e-06

F32 = jnp.float32
BF16 = jnp.bfloat16


def dot(a, b):
    return jnp.dot(a, b, preferred_element_type=F32)


def exact_dot(a, b):
    rows = a.shape[0]
    high = a.astype(BF16)
    rest = a - high.astype(F32)
    mid = rest.astype(BF16)
    low = (rest - mid.astype(F32)).astype(BF16)
    out = dot(jnp.concatenate([high, mid, low], axis=0), b)
    return out[:rows] + (out[rows : 2 * rows] + out[2 * rows :])


def pack_kernel(dest_ref, bank_ref, out_ref, row_ref):
    out_ref[...] = jnp.zeros_like(out_ref)
    row_ref[FLAT:] = jnp.zeros((ROWS - FLAT, LANES), F32)
    for s in range(STORE):
        row_ref[:FLAT] = bank_ref[pl.ds(s, FLAT, stride=STORE), :]
        row_ref[FLAT:] = jnp.full((ROWS - FLAT, LANES), s + 1, F32)
        out_ref[dest_ref[s]] = row_ref[...].astype(BF16)


def pack(bank, dest):
    return pl.pallas_call(
        pack_kernel,
        out_shape=jax.ShapeDtypeStruct((SLOTS, ROWS, LANES), BF16),
        in_specs=[
            pl.BlockSpec(memory_space=pltpu.SMEM),
            pl.BlockSpec(memory_space=pltpu.VMEM),
        ],
        out_specs=pl.BlockSpec(memory_space=pltpu.VMEM),
        scratch_shapes=[pltpu.VMEM((ROWS, LANES), F32)],
        name="pack",
    )(dest, bank)


def slot_sums(values):
    frames, slots, columns = values.shape
    row = lax.broadcasted_iota(jnp.int32, (slots, frames * slots), 0)
    column = lax.broadcasted_iota(jnp.int32, (slots, frames * slots), 1)
    same = jnp.where(lax.rem(column, slots) == row, 1.0, 0.0).astype(BF16)
    return dot(same, values.reshape(frames * slots, columns))


def family_kernel(
    recv_ref,
    front_h,
    expand_h,
    pair_h,
    merge_h,
    squeeze_h,
    excite_h,
    attend_h,
    score_h,
    embed_h,
    lang_h,
    out_ref,
    front_w,
    expand_w,
    pair_w,
    merge_w,
    squeeze_w,
    excite_w,
    attend_w,
    score_w,
    embed_w,
    lang_w,
    sems,
    flat,
    bank,
    front,
    wide,
    joined,
    merged,
    pre,
    attended,
    total,
    first,
    second,
):
    mb = 40
    nb = 256
    copies = [
        pltpu.make_async_copy(source, target, sems.at[i])
        for i, (source, target) in enumerate(
            [
                (front_h, front_w),
                (expand_h, expand_w),
                (pair_h, pair_w),
                (merge_h, merge_w),
                (squeeze_h, squeeze_w),
                (excite_h, excite_w),
                (attend_h, attend_w),
                (score_h, score_w),
                (embed_h, embed_w),
                (lang_h, lang_w),
            ]
        )
    ]
    for copy in copies:
        copy.start()

    for s in range(SLOTS):
        flat[pl.ds(s, ROWS, stride=SLOTS), :] = recv_ref[s].astype(F32)
    header = flat[FLAT * SLOTS : (FLAT + 1) * SLOTS]
    bank[0] = jnp.zeros((SLOTS, WIDE), BF16)
    bank[NSUPER + 1] = jnp.zeros((SLOTS, WIDE), BF16)
    for r in range(NSUPER):
        for t in range(BLOCKS):
            at = (BLOCKS * r + t) * SLOTS
            bank[r + 1, :, t * LANES : (t + 1) * LANES] = flat[at : at + SLOTS].astype(BF16)

    copies[0].wait()

    def front_cols(n, carry):
        cols = pl.ds(pl.multiple_of(n * nb, nb), nb)
        sums = jnp.zeros((SLOTS, nb), F32)
        for j in range(SUPER):
            start = MELS * (j - 2)
            block, offset = start // LANES, start % LANES
            pieces = []
            for t in range(block, block + 4):
                shift, lane = t // BLOCKS, t % BLOCKS
                pieces.append(
                    bank[1 + shift : 1 + shift + NSUPER, :, lane * LANES : (lane + 1) * LANES]
                )
            window = jnp.concatenate(pieces, axis=2).reshape(NSUPER * SLOTS, 4 * LANES)
            top = PAD_TOP - offset
            out = dot(window, front_w[top : top + 4 * LANES, cols])
            out = jnp.maximum(out.astype(BF16), 0.0).reshape(NSUPER, SLOTS, nb)
            front[:, j, :, cols] = out
            sums = sums + slot_sums(out)
        first[:, cols] = sums
        return carry

    lax.fori_loop(0, CH // nb, front_cols, 0)

    frames = front.reshape(FRAMES, SLOTS, CH)

    copies[1].wait()
    edge = jnp.zeros((2, SLOTS, CH), BF16)
    wide[0:2] = edge
    wide[FRAMES + 2 : FRAMES + 4] = edge

    def expand_rows(c, carry):
        f0 = c * mb
        rows = frames[pl.ds(f0, mb)].reshape(mb * SLOTS, CH)
        for n in range(CH // nb):
            cols = slice(n * nb, (n + 1) * nb)
            out = jnp.maximum(dot(rows, expand_w[:, cols]).astype(BF16), 0.0)
            out = out.reshape(mb, SLOTS, nb)
            wide[pl.ds(f0 + 2, mb), :, cols] = out
            if n == 0:
                joined[pl.ds(f0, mb), :, :BR] = out[:, :, :BR]
        return carry

    lax.fori_loop(0, FRAMES // mb, expand_rows, 0)

    copies[2].wait()
    quads = wide.reshape(FRAMES // 4 + 1, 4, SLOTS, CH)
    outs = joined.reshape(FRAMES // 4, 4, SLOTS, CH)
    nq = FRAMES // 4
    for i in range(1, SCALE):
        cols = slice(i * BR, (i + 1) * BR)
        after = slice((i + 1) * BR, (i + 2) * BR)
        rows = jnp.concatenate(
            [
                jnp.concatenate(
                    [
                        quads[:nq, p, :, cols],
                        quads[:nq, p + 2, :, cols],
                        quads[1:, p, :, cols],
                        quads[1:, p + 2, :, cols],
                    ],
                    axis=2,
                )
                for p in range(2)
            ],
            axis=0,
        ).reshape(2 * nq * SLOTS, 4 * BR)
        out = jnp.maximum(dot(rows, pair_w[i - 1]).astype(BF16), 0.0)
        out = out.reshape(2, nq, SLOTS, 2 * BR)
        for p in range(2):
            early, late = out[p, :, :, :BR], out[p, :, :, BR:]
            outs[:, p, :, cols] = early
            outs[:, p + 2, :, cols] = late
            if i < SCALE - 1:
                quads[:nq, p + 2, :, after] = quads[:nq, p + 2, :, after] + early
                quads[1:, p, :, after] = quads[1:, p, :, after] + late

    copies[3].wait()
    total[...] = jnp.zeros_like(total)

    def merge_rows(c, carry):
        f0 = c * mb
        rows = joined[pl.ds(f0, mb)].reshape(mb * SLOTS, CH)
        for n in range(CH // nb):
            cols = slice(n * nb, (n + 1) * nb)
            out = jnp.maximum(dot(rows, merge_w[:, cols]), 0.0).reshape(mb, SLOTS, nb)
            merged[pl.ds(f0, mb), :, cols] = out.astype(BF16)
            total[:, cols] += jnp.sum(out, axis=0)
        return carry

    lax.fori_loop(0, FRAMES // mb, merge_rows, 0)

    for k in range(4, 10):
        copies[k].wait()
    squeezed = total[...] * (1.0 / FRAMES)
    hidden = jnp.maximum(exact_dot(squeezed, squeeze_w[...]), 0.0)
    excited = jax.nn.sigmoid(exact_dot(hidden, excite_w[...]))
    gate = excited.astype(BF16)

    shift = (first[...] * (1.0 / FRAMES) + squeezed * excited).astype(BF16)
    first[...] = jnp.zeros_like(first)
    second[...] = jnp.zeros_like(second)

    def trunk_rows(c, carry):
        f0 = c * mb
        acc = jnp.zeros((mb * SLOTS, ATT), F32)
        for n in range(CH // nb):
            cols = slice(n * nb, (n + 1) * nb)
            out = frames[pl.ds(f0, mb), :, cols] + (
                merged[pl.ds(f0, mb), :, cols] * gate[:, cols][None]
            )
            frames[pl.ds(f0, mb), :, cols] = out
            off = out - shift[:, cols][None]
            first[:, cols] += slot_sums(off)
            second[:, cols] += slot_sums(off * off)
            acc = acc + dot(out.reshape(mb * SLOTS, nb), attend_w[cols, :])
        pre[pl.ds(f0, mb)] = acc.reshape(mb, SLOTS, ATT)
        return carry

    lax.fori_loop(0, FRAMES // mb, trunk_rows, 0)

    drift = first[...] * (1.0 / FRAMES)
    center = shift.astype(F32) + drift
    variance = jnp.maximum(second[...] * (1.0 / FRAMES) - drift * drift, 0.0)
    spread = jnp.sqrt(variance + EPS_STAT)
    context = exact_dot(center, attend_w[CH : 2 * CH]) + exact_dot(spread, attend_w[2 * CH :])
    attended[...] = jnp.tanh(pre[...] + context[None]).astype(BF16)

    first[...] = center
    second[...] = 1.0 / spread

    def pool_cols(n, carry):
        cols = pl.ds(pl.multiple_of(n * nb, nb), nb)
        middle = first[:, cols].astype(BF16)
        scale = second[:, cols].astype(BF16)
        s0 = jnp.zeros((SLOTS, nb), F32)
        s1 = jnp.zeros((SLOTS, nb), F32)
        s2 = jnp.zeros((SLOTS, nb), F32)
        for f0 in range(0, FRAMES, mb):
            rows = attended[f0 : f0 + mb].reshape(mb * SLOTS, ATT)
            energy = dot(rows, score_w[:, cols]).reshape(mb, SLOTS, nb)
            weight = jnp.exp(energy)
            s0 = s0 + jnp.sum(weight, axis=0)
            z = (frames[f0 : f0 + mb, :, cols] - middle[None]) * scale[None]
            wz = weight.astype(BF16) * z
            s1 = s1 + slot_sums(wz)
            s2 = s2 + slot_sums(wz * z)
        m1 = s1 / s0
        m2 = jnp.maximum(s2 / s0 - m1 * m1, 0.0)
        dev = 1.0 / scale.astype(F32)
        first[:, cols] = middle.astype(F32) + m1 * dev
        second[:, cols] = jnp.sqrt(m2 * dev * dev + EPS_STAT)
        return carry

    lax.fori_loop(0, CH // nb, pool_cols, 0)
    pooled = jnp.concatenate([first[...], second[...]], axis=1).astype(BF16)
    embedding = dot(pooled, embed_w[...])
    logits = dot(embedding.astype(BF16), lang_w[...])
    mean_square = jnp.mean(jnp.square(embedding), axis=1, keepdims=True)
    normed = (embedding * lax.rsqrt(mean_square + EPS_NORM)).astype(BF16).astype(F32)
    parts = [
        normed[:, :LANES],
        jnp.concatenate([normed[:, LANES:], jnp.zeros((SLOTS, 2 * LANES - EMB), F32)], axis=1),
        jnp.concatenate([logits, jnp.zeros((SLOTS, LANES - LANGS), F32)], axis=1),
        header,
    ]
    for k, part in enumerate(parts):
        for m in range(8):
            out_ref[pl.ds(4 * m + k, SLOTS, stride=32), :] = part


def family(recv, weights):
    vmem = pl.BlockSpec(memory_space=pltpu.VMEM)
    away = pl.BlockSpec(memory_space=pl.ANY)
    return pl.pallas_call(
        family_kernel,
        out_shape=jax.ShapeDtypeStruct((SLOTS * 8 * 4, LANES), F32),
        in_specs=[vmem] + [away] * len(weights),
        out_specs=vmem,
        scratch_shapes=[pltpu.VMEM(w.shape, w.dtype) for w in weights]
        + [
            pltpu.SemaphoreType.DMA((len(weights),)),
            pltpu.VMEM((ROWS * SLOTS, LANES), F32),
            pltpu.VMEM((NSUPER + 2, SLOTS, WIDE), BF16),
            pltpu.VMEM((NSUPER, SUPER, SLOTS, CH), BF16),
            pltpu.VMEM((FRAMES + 4, SLOTS, CH), BF16),
            pltpu.VMEM((FRAMES, SLOTS, CH), BF16),
            pltpu.VMEM((FRAMES, SLOTS, CH), BF16),
            pltpu.VMEM((FRAMES, SLOTS, ATT), F32),
            pltpu.VMEM((FRAMES, SLOTS, ATT), BF16),
            pltpu.VMEM((SLOTS, CH), F32),
            pltpu.VMEM((SLOTS, CH), F32),
            pltpu.VMEM((SLOTS, CH), F32),
        ],
        compiler_params=pltpu.CompilerParams(vmem_limit_bytes=52 << 20),
        cost_estimate=pl.CostEstimate(
            flops=20_000_000_000, bytes_accessed=10_000_000, transcendentals=4_000_000
        ),
        name="family",
    )(recv, *weights)


def home_kernel(mem_ref, recv_ref, logits_ref, sim_ref, held):
    rows = recv_ref.shape[0] // 4
    head0, head1, tail, mark = (recv_ref[pl.ds(k, rows, stride=4), :] for k in range(4))
    row = lax.broadcasted_iota(jnp.int32, (rows, LANES), 0)
    lane = lax.broadcasted_iota(jnp.int32, (rows, LANES), 1)
    place = lax.rem(row, 8) * STORE + mark.astype(jnp.int32) - 1
    pick = jnp.where((mark > 0.5) & (place == lane), 1.0, 0.0)
    pick16 = pick.astype(BF16)
    turned = (((0,), (0,)), ((), ()))
    normed = lax.dot_general(
        pick16,
        jnp.concatenate([head0, head1], axis=1).astype(BF16),
        turned,
        preferred_element_type=F32,
    )
    held[:, : 2 * LANES] = normed
    held[:, 2 * LANES :] = lax.dot_general(
        pick, tail, turned, preferred_element_type=F32, precision=lax.Precision.HIGHEST
    )
    own = held[pl.ds(pl.multiple_of(mem_ref[0] * STORE, STORE), STORE)]
    logits_ref[0] = own[:, 2 * LANES : 2 * LANES + LANGS]
    sim = lax.dot_general(
        own[:, : 2 * LANES].astype(BF16),
        normed[: 8 * STORE].astype(BF16),
        (((1,), (1,)), ((), ())),
        preferred_element_type=F32,
    )
    sim_ref[0] = sim / EMB


def home(member, recv):
    vmem = pl.BlockSpec(memory_space=pltpu.VMEM)
    return pl.pallas_call(
        home_kernel,
        out_shape=(
            jax.ShapeDtypeStruct((1, STORE, LANGS), F32),
            jax.ShapeDtypeStruct((1, STORE, 8 * STORE), F32),
        ),
        in_specs=[pl.BlockSpec(memory_space=pltpu.SMEM), vmem],
        out_specs=(vmem, vmem),
        scratch_shapes=[pltpu.VMEM((LANES, 3 * LANES), F32)],
        name="home",
    )(member, recv)


def prepare(initial_conv_weight, branch_weight):
    tall = jnp.pad(initial_conv_weight, ((PAD_TOP, PAD_TOP), (0, 0)))
    early = jnp.pad(branch_weight, ((0, 0), (0, BR), (0, 0)))
    late = jnp.pad(branch_weight, ((0, 0), (BR, 0), (0, 0)))
    return tall, jnp.concatenate([early, late], axis=2)


def shards(
    filterbank,
    destination,
    initial_conv_weight,
    expand_weight,
    branch_weight,
    merge_weight,
    squeeze_weight,
    excite_weight,
    attend_weight,
    score_weight,
    embed_weight,
    language_weight,
):
    bank = filterbank.reshape(STORE, FLAT, LANES).transpose(1, 0, 2).reshape(FLAT * STORE, LANES)
    outbound = pack(bank, destination.reshape(STORE))
    arrived = lax.all_to_all(outbound, "grp", split_axis=0, concat_axis=0, tiled=True)
    tall, pairs = prepare(initial_conv_weight, branch_weight)
    scored = family(
        arrived,
        (
            tall,
            expand_weight,
            pairs,
            merge_weight,
            squeeze_weight,
            excite_weight,
            attend_weight[0],
            score_weight[0],
            embed_weight[0],
            language_weight[0],
        ),
    )
    back = lax.all_to_all(
        scored.reshape(SLOTS * 8, 4, LANES),
        ("grp", "mem"),
        split_axis=0,
        concat_axis=0,
        tiled=True,
    )
    member = lax.axis_index("mem").astype(jnp.int32).reshape(1)
    return home(member, back.reshape(SLOTS * 8 * 4, LANES))


def solution(mesh):
    return jax.shard_map(
        shards,
        mesh=mesh,
        in_specs=(
            P("grp", "mem", None, None),
            P("grp", "mem"),
            P(),
            P(),
            P(),
            P(),
            P(),
            P(),
            P("grp", None, None),
            P("grp", None, None),
            P("grp", None, None),
            P("grp", None, None),
        ),
        out_specs=(P("grp", "mem", None), P("grp", "mem", None)),
        check_vma=False,
    )
```

time: 96.4 us -> 83.4 us (0.87)
  Pallas kernels: 56.5 us -> 44.2 us
    pallas_call x1, Pallas kernels: 52.1 us -> 40.1 us  [family(): pl.pallas_call(family_kernel, out_shape=jax.ShapeDtypeStruct((SLOTS * 8 *...]
    unnamed x11 -> x17, local copies, waits for them, and re-layouts: 2.81 us -> 2.03 us
  transfers between devices with their start and end apart: 2 -> 2, of which waited for: 2 -> 2; matrix products, arithmetic and copies ran while one was open for 4% -> 5% of each run, Pallas kernels for 0% -> 0%
where the time goes in v1:
time: 83.4 us; the launch traced here: 83.1 us
  Pallas kernels  44.2 us (53%)
  waiting for transfers between devices  17.2 us (21%)
  starting transfers between devices  16.2 us (19%)
  local copies, waits for them, and re-layouts  3.25 us (4%)
  other arithmetic  1.47 us (2%)
    pallas_call x1, Pallas kernels, family(): pl.pallas_call(family_kernel, out_shape=jax.ShapeDtypeStruct((SLOTS * 8 *...  40.1 us
    all_to_all x1, waiting for transfers between devices, shards(): lax.all_to_all(scored.reshape(SLOTS * 8, 4, LANES), ('grp', 'mem'), split...  10.9 us
    all_to_all x1, starting transfers between devices, shards(): lax.all_to_all(scored.reshape(SLOTS * 8, 4, LANES), ('grp', 'mem'), split...  8.6 us
    all_to_all x1, starting transfers between devices, shards(): lax.all_to_all(outbound, 'grp', split_axis=0, concat_axis=0, tiled=True)  7.58 us
    all_to_all x1, waiting for transfers between devices, shards(): lax.all_to_all(outbound, 'grp', split_axis=0, concat_axis=0, tiled=True)  6.27 us
    pallas_call x1, Pallas kernels, pack(): pl.pallas_call(pack_kernel, out_shape=jax.ShapeDtypeStruct((SLOTS, ROWS,...  2.15 us
    unnamed x17, local copies, waits for them, and re-layouts  2.03 us
    pallas_call x1, Pallas kernels, home(): pl.pallas_call(home_kernel, out_shape=(jax.ShapeDtypeStruct((1, STORE, LA...  1.94 us
  transfers between devices with their start and end apart: 2, of which 2 were waited for; matrix products, arithmetic and copies ran while one was open for 5% of the time, Pallas kernels for 0%

profile of v1, /device:TPU:1, one launch (start us, length us, event | category | flops | bytes accessed | tf_op | source)
XLA Modules:
  0.0 83.1 jit_solution(13462098097540598183)
XLA Ops:
  0.6 0.0 copy-start.6
  0.6 0.0 copy-start.5
  0.7 2.1 %pack.1 = bf16[16,128,128]{2,1,0:T(8,128)(2,1)} custom-call(s32[8]{0:T(128)} %bitcast.18, f32[1000,128]{1,0:T(8,128)} %bitcast.17), custom_call_target="tpu_custom_call" | custom-call | tf_op jit(solution)/shard_map/pack/pallas_call | solution.py:63
  2.8 7.6 %all-to-all-start = ((bf16[16,128,128]{2,1,0:T(8,128)(2,1)}), bf16[16,128,128]{2,1,0:T(8,128)(2,1)S(1)}, u32[]{:S(2)}, u32[]{:S(2)}) async-start(bf16[16,128,128]{2,1,0:T(8,128)(2,1)} %pack.1), calls=%async_computation | async-start | bytes 1048576 | tf_op jit(solution)/shard_map/all_to_all | solution.py:423
  10.4 0.0 copy-done.6
  10.4 0.0 copy-start.7
  10.4 1.3 %copy.14 = bf16[1,2048,192]{2,1,0:T(8,128)(2,1)} copy(bf16[1,2048,192]{1,2,0:T(8,128)(2,1)S(1)} %copy-done.6) | data formatting | bytes 1572864 | tf_op args[10]
  11.7 0.0 copy-done.5
  11.7 0.0 copy-start
  11.7 0.0 copy-start.1
  11.7 0.0 copy-start.3
  11.7 1.2 %pad.12.front_h = bf16[624,1024]{1,0:T(8,128)(2,1)} pad(bf16[400,1024]{1,0:T(8,128)(2,1)S(1)} %copy-done.5, bf16[]{:T(256)} %constant.6.clone.1), padding=112_112x0_0 | pad | bytes 2097154 | tf_op jit(solution)/shard_map/jit(_pad)/pad | solution.py:401
  12.9 0.0 copy-done.7
  12.9 1.5 %fusion.2.pair_h = bf16[7,512,256]{2,1,0:T(8,128)(2,1)} fusion(bf16[7,384,128]{2,1,0:T(8,128)(2,1)S(1)} %copy-done.7), kind=kLoop, calls=%fused_computation.4 | loop fusion | flops 7340032 | bytes 2523136 | tf_op jit(solution)/shard_map/concatenate | solution.py:404
  14.4 6.3 %all-to-all-done.recv_ref = bf16[16,128,128]{2,1,0:T(8,128)(2,1)S(1)} async-done(((bf16[16,128,128]{2,1,0:T(8,128)(2,1)}), bf16[16,128,128]{2,1,0:T(8,128)(2,1)S(1)}, u32[]{:S(2)}, u32[]{:S(2)}) %all-to-all-start) | async-done | bytes 524320 | tf_op jit(solution)/shard_map/all_to_all | solution.py:423
  20.7 0.0 copy-done
  20.7 0.0 copy-done.1
  20.7 0.0 copy-done.2
  20.7 0.0 copy-done.3
  20.7 40.1 %family.1 = f32[512,128]{1,0:T(8,128)} custom-call(bf16[16,128,128]{2,1,0:T(8,128)(2,1)S(1)} %all-to-all-done.recv_ref, bf16[624,1024]{1,0:T(8,128)(2,1)} %pad.12.front_h, bf16[1024,1024]{1,0:T(8,128)(2,1)} %expand_h.1, bf16[7,512,256]{2,1,0:T(8,128)(2,1)} %fusion.2.pair_h, bf16[1024,1024]{1,0:T(8,128)(2,1)} %merge_h.1, bf16[1024,128]{1,0:T(8,128)(2,1)S(1)} %copy-done, ...), custom_call_target="tpu_custom_call" | custom-call | flops 20000000000 | bytes 10000000 | tf_op jit(solution)/shard_map/family/pallas_call | solution.py:327
  60.9 8.6 %all-to-all-start.1 = ((f32[128,4,128]{2,1,0:T(4,128)}), f32[128,4,128]{2,1,0:T(4,128)S(1)}, u32[]{:S(2)}, u32[]{:S(2)}) async-start(f32[128,4,128]{2,1,0:T(4,128)} %bitcast.9), calls=%async_computation.1 | async-start | bytes 524288 | tf_op jit(solution)/shard_map/all_to_all | solution.py:440
  69.5 10.9 %all-to-all-done.1 = f32[128,4,128]{2,1,0:T(4,128)S(1)} async-done(((f32[128,4,128]{2,1,0:T(4,128)}), f32[128,4,128]{2,1,0:T(4,128)S(1)}, u32[]{:S(2)}, u32[]{:S(2)}) %all-to-all-start.1) | async-done | bytes 262176 | tf_op jit(solution)/shard_map/all_to_all | solution.py:440
  80.4 0.7 copy-done.4
  81.1 1.9 %home.1 = (f32[1,8,107]{2,1,0:T(8,128)}, f32[1,8,64]{2,1,0:T(8,128)}) custom-call(s32[1]{0:T(128)} %bitcast.mem_ref, f32[512,128]{1,0:T(8,128)} %bitcast.16), custom_call_target="tpu_custom_call" | custom-call | tf_op jit(solution)/shard_map/home/pallas_call | solution.py:387
  (2 shorter events, 0.0 us)
Async XLA Ops:
  0.6 9.8 %copy-start.6 = (bf16[1,2048,192]{1,2,0:T(8,128)(2,1)S(1)}, bf16[1,2048,192]{1,2,0:T(8,128)(2,1)}, u32[]{:S(2)}) copy-start(bf16[1,2048,192]{1,2,0:T(8,128)(2,1)} %param.22) | copy-start | bytes 2359300
  0.6 11.1 %copy-start.5 = (bf16[400,1024]{1,0:T(8,128)(2,1)S(1)}, bf16[400,1024]{1,0:T(8,128)(2,1)}, u32[]{:S(2)}) copy-start(bf16[400,1024]{1,0:T(8,128)(2,1)} %param.14) | copy-start | bytes 2457604
  2.8 17.9 %all-to-all-start = ((bf16[16,128,128]{2,1,0:T(8,128)(2,1)}), bf16[16,128,128]{2,1,0:T(8,128)(2,1)S(1)}, u32[]{:S(2)}, u32[]{:S(2)}) async-start(bf16[16,128,128]{2,1,0:T(8,128)(2,1)} %pack.1), calls=%async_computation | async-start | bytes 1048576 | tf_op jit(solution)/shard_map/all_to_all | solution.py:423
  10.4 2.5 %copy-start.7 = (bf16[7,384,128]{2,1,0:T(8,128)(2,1)S(1)}, bf16[7,384,128]{2,1,0:T(8,128)(2,1)}, u32[]{:S(2)}) copy-start(bf16[7,384,128]{2,1,0:T(8,128)(2,1)} %param.16) | copy-start | bytes 2064388
  11.7 9.0 %copy-start = (bf16[1024,128]{1,0:T(8,128)(2,1)S(1)}, bf16[1024,128]{1,0:T(8,128)(2,1)}, u32[]{:S(2)}) copy-start(bf16[1024,128]{1,0:T(8,128)(2,1)} %squeeze_h.1) | copy-start | bytes 786436
  11.7 9.0 %copy-start.1 = (bf16[128,1024]{1,0:T(8,128)(2,1)S(1)}, bf16[128,1024]{1,0:T(8,128)(2,1)}, u32[]{:S(2)}) copy-start(bf16[128,1024]{1,0:T(8,128)(2,1)} %excite_h.1) | copy-start | bytes 786436
  11.7 9.0 %copy-start.2 = (bf16[1,128,1024]{2,1,0:T(8,128)(2,1)S(1)}, bf16[1,128,1024]{2,1,0:T(8,128)(2,1)}, u32[]{:S(2)}) copy-start(bf16[1,128,1024]{2,1,0:T(8,128)(2,1)} %param.21) | copy-start | bytes 786436
  11.7 9.0 %copy-start.3 = (bf16[1,192,107]{2,1,0:T(8,128)(2,1)S(1)}, bf16[1,192,107]{2,1,0:T(8,128)(2,1)}, u32[]{:S(2)}) copy-start(bf16[1,192,107]{2,1,0:T(8,128)(2,1)} %param.23) | copy-start | bytes 123268
  60.9 19.5 %all-to-all-start.1 = ((f32[128,4,128]{2,1,0:T(4,128)}), f32[128,4,128]{2,1,0:T(4,128)S(1)}, u32[]{:S(2)}, u32[]{:S(2)}) async-start(f32[128,4,128]{2,1,0:T(4,128)} %bitcast.9), calls=%async_computation.1 | async-start | bytes 524288 | tf_op jit(solution)/shard_map/all_to_all | solution.py:440
  80.4 0.7 copy-start.4

commit v2 on v1

--- a/solution.py
+++ b/solution.py
@@ -69,6 +69,7 @@
         ],
         out_specs=pl.BlockSpec(memory_space=pltpu.VMEM),
         scratch_shapes=[pltpu.VMEM((ROWS, LANES), F32)],
+        compiler_params=pltpu.CompilerParams(vmem_limit_bytes=16 << 20),
         name="pack",
     )(dest, bank)
 
@@ -79,6 +80,21 @@
     column = lax.broadcasted_iota(jnp.int32, (slots, frames * slots), 1)
     same = jnp.where(lax.rem(column, slots) == row, 1.0, 0.0).astype(BF16)
     return dot(same, values.reshape(frames * slots, columns))
+
+
+def fours(values):
+    frames, slots, columns = values.shape
+    split = values.reshape(frames // 4, 4, slots, columns)
+    return (split[:, 0] + split[:, 1]) + (split[:, 2] + split[:, 3])
+
+
+def get(ref, frames, blocks):
+    return jnp.concatenate([ref[frames, k] for k in blocks], axis=-1)
+
+
+def put(ref, frames, blocks, values):
+    for i, k in enumerate(blocks):
+        ref[frames, k] = values[..., i * LANES : (i + 1) * LANES]
 
 
 def family_kernel(
@@ -142,101 +158,106 @@
     for s in range(SLOTS):
         flat[pl.ds(s, ROWS, stride=SLOTS), :] = recv_ref[s].astype(F32)
     header = flat[FLAT * SLOTS : (FLAT + 1) * SLOTS]
-    bank[0] = jnp.zeros((SLOTS, WIDE), BF16)
-    bank[NSUPER + 1] = jnp.zeros((SLOTS, WIDE), BF16)
-    for r in range(NSUPER):
-        for t in range(BLOCKS):
-            at = (BLOCKS * r + t) * SLOTS
-            bank[r + 1, :, t * LANES : (t + 1) * LANES] = flat[at : at + SLOTS].astype(BF16)
+    bank[0] = jnp.zeros((BLOCKS, SLOTS, LANES), BF16)
+    bank[NSUPER + 1] = jnp.zeros((BLOCKS, SLOTS, LANES), BF16)
+    bank[1 : NSUPER + 1] = (
+        flat[: FLAT * SLOTS].astype(BF16).reshape(NSUPER, BLOCKS, SLOTS, LANES)
+    )
 
     copies[0].wait()
+
+    nk = nb // LANES
 
     def front_cols(n, carry):
         cols = pl.ds(pl.multiple_of(n * nb, nb), nb)
-        sums = jnp.zeros((SLOTS, nb), F32)
+        blocks = [n * nk + k for k in range(nk)]
         for j in range(SUPER):
             start = MELS * (j - 2)
             block, offset = start // LANES, start % LANES
-            pieces = []
-            for t in range(block, block + 4):
-                shift, lane = t // BLOCKS, t % BLOCKS
-                pieces.append(
-                    bank[1 + shift : 1 + shift + NSUPER, :, lane * LANES : (lane + 1) * LANES]
-                )
-            window = jnp.concatenate(pieces, axis=2).reshape(NSUPER * SLOTS, 4 * LANES)
+            window = jnp.concatenate(
+                [
+                    bank[1 + t // BLOCKS : 1 + t // BLOCKS + NSUPER, t % BLOCKS]
+                    for t in range(block, block + 4)
+                ],
+                axis=2,
+            ).reshape(NSUPER * SLOTS, 4 * LANES)
             top = PAD_TOP - offset
             out = dot(window, front_w[top : top + 4 * LANES, cols])
+            if j == 0:
+                sample = jnp.maximum(out, 0.0).reshape(NSUPER, SLOTS, nb)
+                first[:, cols] = jnp.sum(sample, axis=0) * (1.0 / NSUPER)
             out = jnp.maximum(out.astype(BF16), 0.0).reshape(NSUPER, SLOTS, nb)
-            front[:, j, :, cols] = out
-            sums = sums + slot_sums(out)
-        first[:, cols] = sums
+            for i, k in enumerate(blocks):
+                front[:, j, k] = out[:, :, i * LANES : (i + 1) * LANES]
         return carry
 
     lax.fori_loop(0, CH // nb, front_cols, 0)
 
-    frames = front.reshape(FRAMES, SLOTS, CH)
+    nf = CH // LANES
+    frames = front.reshape(FRAMES, nf, SLOTS, LANES)
 
     copies[1].wait()
-    edge = jnp.zeros((2, SLOTS, CH), BF16)
+    edge = jnp.zeros((2, nf, SLOTS, LANES), BF16)
     wide[0:2] = edge
     wide[FRAMES + 2 : FRAMES + 4] = edge
 
     def expand_rows(c, carry):
         f0 = c * mb
-        rows = frames[pl.ds(f0, mb)].reshape(mb * SLOTS, CH)
+        rows = get(frames, pl.ds(f0, mb), range(nf)).reshape(mb * SLOTS, CH)
         for n in range(CH // nb):
             cols = slice(n * nb, (n + 1) * nb)
             out = jnp.maximum(dot(rows, expand_w[:, cols]).astype(BF16), 0.0)
             out = out.reshape(mb, SLOTS, nb)
-            wide[pl.ds(f0 + 2, mb), :, cols] = out
+            put(wide, pl.ds(f0 + 2, mb), range(n * nk, (n + 1) * nk), out)
             if n == 0:
-                joined[pl.ds(f0, mb), :, :BR] = out[:, :, :BR]
+                joined[pl.ds(f0, mb), 0] = out[:, :, :BR]
         return carry
 
     lax.fori_loop(0, FRAMES // mb, expand_rows, 0)
 
     copies[2].wait()
-    quads = wide.reshape(FRAMES // 4 + 1, 4, SLOTS, CH)
-    outs = joined.reshape(FRAMES // 4, 4, SLOTS, CH)
     nq = FRAMES // 4
+    quads = wide.reshape(nq + 1, 4, nf, SLOTS, LANES)
+    outs = joined.reshape(nq, 4, nf, SLOTS, LANES)
     for i in range(1, SCALE):
-        cols = slice(i * BR, (i + 1) * BR)
-        after = slice((i + 1) * BR, (i + 2) * BR)
-        rows = jnp.concatenate(
-            [
-                jnp.concatenate(
-                    [
-                        quads[:nq, p, :, cols],
-                        quads[:nq, p + 2, :, cols],
-                        quads[1:, p, :, cols],
-                        quads[1:, p + 2, :, cols],
-                    ],
-                    axis=2,
-                )
-                for p in range(2)
-            ],
-            axis=0,
-        ).reshape(2 * nq * SLOTS, 4 * BR)
-        out = jnp.maximum(dot(rows, pair_w[i - 1]).astype(BF16), 0.0)
-        out = out.reshape(2, nq, SLOTS, 2 * BR)
-        for p in range(2):
-            early, late = out[p, :, :, :BR], out[p, :, :, BR:]
-            outs[:, p, :, cols] = early
-            outs[:, p + 2, :, cols] = late
-            if i < SCALE - 1:
-                quads[:nq, p + 2, :, after] = quads[:nq, p + 2, :, after] + early
-                quads[1:, p, :, after] = quads[1:, p, :, after] + late
+        cut = nq // 2 + SCALE // 2 - i
+        for lo, hi in ((0, cut), (cut, nq)):
+            n = hi - lo
+            rows = jnp.concatenate(
+                [
+                    jnp.concatenate(
+                        [
+                            quads[lo:hi, p, i],
+                            quads[lo:hi, p + 2, i],
+                            quads[lo + 1 : hi + 1, p, i],
+                            quads[lo + 1 : hi + 1, p + 2, i],
+                        ],
+                        axis=2,
+                    )
+                    for p in range(2)
+                ],
+                axis=0,
+            ).reshape(2 * n * SLOTS, 4 * BR)
+            out = jnp.maximum(dot(rows, pair_w[i - 1]).astype(BF16), 0.0)
+            out = out.reshape(2, n, SLOTS, 2 * BR)
+            for p in range(2):
+                early, late = out[p, :, :, :BR], out[p, :, :, BR:]
+                outs[lo:hi, p, i] = early
+                outs[lo:hi, p + 2, i] = late
+                if i < SCALE - 1:
+                    quads[lo:hi, p + 2, i + 1] = quads[lo:hi, p + 2, i + 1] + early
+                    quads[lo + 1 : hi + 1, p, i + 1] = quads[lo + 1 : hi + 1, p, i + 1] + late
 
     copies[3].wait()
     total[...] = jnp.zeros_like(total)
 
     def merge_rows(c, carry):
         f0 = c * mb
-        rows = joined[pl.ds(f0, mb)].reshape(mb * SLOTS, CH)
+        rows = get(joined, pl.ds(f0, mb), range(nf)).reshape(mb * SLOTS, CH)
         for n in range(CH // nb):
             cols = slice(n * nb, (n + 1) * nb)
             out = jnp.maximum(dot(rows, merge_w[:, cols]), 0.0).reshape(mb, SLOTS, nb)
-            merged[pl.ds(f0, mb), :, cols] = out.astype(BF16)
+            put(merged, pl.ds(f0, mb), range(n * nk, (n + 1) * nk), out.astype(BF16))
             total[:, cols] += jnp.sum(out, axis=0)
         return carry
 
@@ -249,7 +270,7 @@
     excited = jax.nn.sigmoid(exact_dot(hidden, excite_w[...]))
     gate = excited.astype(BF16)
 
-    shift = (first[...] * (1.0 / FRAMES) + squeezed * excited).astype(BF16)
+    shift = (first[...] + squeezed * excited).astype(BF16)
     first[...] = jnp.zeros_like(first)
     second[...] = jnp.zeros_like(second)
 
@@ -258,13 +279,14 @@
         acc = jnp.zeros((mb * SLOTS, ATT), F32)
         for n in range(CH // nb):
             cols = slice(n * nb, (n + 1) * nb)
-            out = frames[pl.ds(f0, mb), :, cols] + (
-                merged[pl.ds(f0, mb), :, cols] * gate[:, cols][None]
+            blocks = range(n * nk, (n + 1) * nk)
+            out = get(frames, pl.ds(f0, mb), blocks) + (
+                get(merged, pl.ds(f0, mb), blocks) * gate[:, cols][None]
             )
-            frames[pl.ds(f0, mb), :, cols] = out
+            put(frames, pl.ds(f0, mb), blocks, out)
             off = out - shift[:, cols][None]
-            first[:, cols] += slot_sums(off)
-            second[:, cols] += slot_sums(off * off)
+            first[:, cols] += slot_sums(fours(off))
+            second[:, cols] += slot_sums(fours(off * off))
             acc = acc + dot(out.reshape(mb * SLOTS, nb), attend_w[cols, :])
         pre[pl.ds(f0, mb)] = acc.reshape(mb, SLOTS, ATT)
         return carry
@@ -281,44 +303,42 @@
     first[...] = center
     second[...] = 1.0 / spread
 
-    def pool_cols(n, carry):
-        cols = pl.ds(pl.multiple_of(n * nb, nb), nb)
+    for n in range(CH // nb):
+        cols = slice(n * nb, (n + 1) * nb)
+        blocks = range(n * nk, (n + 1) * nk)
         middle = first[:, cols].astype(BF16)
         scale = second[:, cols].astype(BF16)
-        s0 = jnp.zeros((SLOTS, nb), F32)
-        s1 = jnp.zeros((SLOTS, nb), F32)
-        s2 = jnp.zeros((SLOTS, nb), F32)
+        parts = []
         for f0 in range(0, FRAMES, mb):
             rows = attended[f0 : f0 + mb].reshape(mb * SLOTS, ATT)
             energy = dot(rows, score_w[:, cols]).reshape(mb, SLOTS, nb)
-            weight = jnp.exp(energy)
-            s0 = s0 + jnp.sum(weight, axis=0)
-            z = (frames[f0 : f0 + mb, :, cols] - middle[None]) * scale[None]
-            wz = weight.astype(BF16) * z
-            s1 = s1 + slot_sums(wz)
-            s2 = s2 + slot_sums(wz * z)
+            weight = jnp.exp(energy).astype(BF16)
+            z = (get(frames, slice(f0, f0 + mb), blocks) - middle[None]) * scale[None]
+            wz = weight * z
+            parts.append((fours(weight), fours(wz), fours(wz * z)))
+        s0, s1, s2 = (slot_sums(jnp.concatenate(part, axis=0)) for part in zip(*parts))
         m1 = s1 / s0
         m2 = jnp.maximum(s2 / s0 - m1 * m1, 0.0)
         dev = 1.0 / scale.astype(F32)
         first[:, cols] = middle.astype(F32) + m1 * dev
         second[:, cols] = jnp.sqrt(m2 * dev * dev + EPS_STAT)
-        return carry
-
-    lax.fori_loop(0, CH // nb, pool_cols, 0)
     pooled = jnp.concatenate([first[...], second[...]], axis=1).astype(BF16)
     embedding = dot(pooled, embed_w[...])
     logits = dot(embedding.astype(BF16), lang_w[...])
     mean_square = jnp.mean(jnp.square(embedding), axis=1, keepdims=True)
     normed = (embedding * lax.rsqrt(mean_square + EPS_NORM)).astype(BF16).astype(F32)
+    high = logits.astype(BF16).astype(F32)
+    fill = jnp.zeros((SLOTS, LANES - LANGS), F32)
     parts = [
         normed[:, :LANES],
-        jnp.concatenate([normed[:, LANES:], jnp.zeros((SLOTS, 2 * LANES - EMB), F32)], axis=1),
-        jnp.concatenate([logits, jnp.zeros((SLOTS, LANES - LANGS), F32)], axis=1),
-        header,
+        jnp.concatenate([normed[:, LANES:], header[:, : 2 * LANES - EMB]], axis=1),
+        jnp.concatenate([high, fill], axis=1),
+        jnp.concatenate([logits - high, fill], axis=1),
     ]
     for k, part in enumerate(parts):
         for m in range(8):
-            out_ref[pl.ds(4 * m + k, SLOTS, stride=32), :] = part
+            flat[pl.ds(4 * m + k, SLOTS, stride=32), :] = part
+    out_ref[...] = flat[: SLOTS * 32].astype(BF16)
 
 
 def family(recv, weights):
@@ -326,18 +346,18 @@
     away = pl.BlockSpec(memory_space=pl.ANY)
     return pl.pallas_call(
         family_kernel,
-        out_shape=jax.ShapeDtypeStruct((SLOTS * 8 * 4, LANES), F32),
+        out_shape=jax.ShapeDtypeStruct((SLOTS * 8 * 4, LANES), BF16),
         in_specs=[vmem] + [away] * len(weights),
         out_specs=vmem,
         scratch_shapes=[pltpu.VMEM(w.shape, w.dtype) for w in weights]
         + [
             pltpu.SemaphoreType.DMA((len(weights),)),
             pltpu.VMEM((ROWS * SLOTS, LANES), F32),
-            pltpu.VMEM((NSUPER + 2, SLOTS, WIDE), BF16),
-            pltpu.VMEM((NSUPER, SUPER, SLOTS, CH), BF16),
-            pltpu.VMEM((FRAMES + 4, SLOTS, CH), BF16),
-            pltpu.VMEM((FRAMES, SLOTS, CH), BF16),
-            pltpu.VMEM((FRAMES, SLOTS, CH), BF16),
+            pltpu.VMEM((NSUPER + 2, BLOCKS, SLOTS, LANES), BF16),
+            pltpu.VMEM((NSUPER, SUPER, CH // LANES, SLOTS, LANES), BF16),
+            pltpu.VMEM((FRAMES + 4, CH // LANES, SLOTS, LANES), BF16),
+            pltpu.VMEM((FRAMES, CH // LANES, SLOTS, LANES), BF16),
+            pltpu.VMEM((FRAMES, CH // LANES, SLOTS, LANES), BF16),
             pltpu.VMEM((FRAMES, SLOTS, ATT), F32),
             pltpu.VMEM((FRAMES, SLOTS, ATT), BF16),
             pltpu.VMEM((SLOTS, CH), F32),
@@ -352,30 +372,27 @@
     )(recv, *weights)
 
 
-def home_kernel(mem_ref, recv_ref, logits_ref, sim_ref, held):
+def home_kernel(mem_ref, recv_ref, logits_ref, sim_ref, flat, held):
     rows = recv_ref.shape[0] // 4
-    head0, head1, tail, mark = (recv_ref[pl.ds(k, rows, stride=4), :] for k in range(4))
+    flat[...] = recv_ref[...].astype(F32)
+    parts = [flat[pl.ds(k, rows, stride=4), :] for k in range(4)]
+    mark = parts[1][:, LANES - 1 :]
     row = lax.broadcasted_iota(jnp.int32, (rows, LANES), 0)
     lane = lax.broadcasted_iota(jnp.int32, (rows, LANES), 1)
     place = lax.rem(row, 8) * STORE + mark.astype(jnp.int32) - 1
-    pick = jnp.where((mark > 0.5) & (place == lane), 1.0, 0.0)
-    pick16 = pick.astype(BF16)
-    turned = (((0,), (0,)), ((), ()))
-    normed = lax.dot_general(
-        pick16,
-        jnp.concatenate([head0, head1], axis=1).astype(BF16),
-        turned,
+    pick = jnp.where((mark > 0.5) & (place == lane), 1.0, 0.0).astype(BF16)
+    held[...] = lax.dot_general(
+        pick,
+        jnp.concatenate(parts, axis=1).astype(BF16),
+        (((0,), (0,)), ((), ())),
         preferred_element_type=F32,
     )
-    held[:, : 2 * LANES] = normed
-    held[:, 2 * LANES :] = lax.dot_general(
-        pick, tail, turned, preferred_element_type=F32, precision=lax.Precision.HIGHEST
-    )
     own = held[pl.ds(pl.multiple_of(mem_ref[0] * STORE, STORE), STORE)]
-    logits_ref[0] = own[:, 2 * LANES : 2 * LANES + LANGS]
+    logits = own[:, 2 * LANES : 3 * LANES] + own[:, 3 * LANES :]
+    logits_ref[0] = logits[:, :LANGS]
     sim = lax.dot_general(
-        own[:, : 2 * LANES].astype(BF16),
-        normed[: 8 * STORE].astype(BF16),
+        own[:, :EMB].astype(BF16),
+        held[: 8 * STORE, :EMB].astype(BF16),
         (((1,), (1,)), ((), ())),
         preferred_element_type=F32,
     )
@@ -392,7 +409,11 @@
         ),
         in_specs=[pl.BlockSpec(memory_space=pltpu.SMEM), vmem],
         out_specs=(vmem, vmem),
-        scratch_shapes=[pltpu.VMEM((LANES, 3 * LANES), F32)],
+        scratch_shapes=[
+            pltpu.VMEM(recv.shape, F32),
+            pltpu.VMEM((LANES, 4 * LANES), F32),
+        ],
+        compiler_params=pltpu.CompilerParams(vmem_limit_bytes=16 << 20),
         name="home",
     )(member, recv)
 

time: 83.4 us -> 75.5 us (0.905)
  Pallas kernels: 44.2 us -> 36.5 us
  waiting for transfers between devices: 17.2 us -> 16 us
  local copies, waits for them, and re-layouts: 3.25 us -> 4.23 us
    pallas_call x1, Pallas kernels: 40.1 us -> 34 us  [family(): pl.pallas_call(family_kernel, out_shape=jax.ShapeDtypeStruct((SLOTS * 8 *...]
    all_to_all x1, waiting for transfers between devices: 10.9 us -> 9.75 us  [shards(): lax.all_to_all(scored.reshape(SLOTS * 8, 4, LANES), ('grp', 'mem'), split...]
    unnamed x17 -> x19, local copies, waits for them, and re-layouts: 2.03 us -> 3 us
    pallas_call x1, Pallas kernels: 1.94 us -> 1.02 us  [home(): pl.pallas_call(home_kernel, out_shape=(jax.ShapeDtypeStruct((1, STORE, LA...]
where the time goes in v2:
time: 75.5 us; the launch traced here: 75.2 us
  Pallas kernels  36.5 us (48%)
  starting transfers between devices  16.2 us (21%)
  waiting for transfers between devices  16 us (21%)
  local copies, waits for them, and re-layouts  4.23 us (6%)
  other arithmetic  1.46 us (2%)
    pallas_call x1, Pallas kernels, family(): pl.pallas_call(family_kernel, out_shape=jax.ShapeDtypeStruct((SLOTS * 8 *...  34 us
    all_to_all x1, waiting for transfers between devices, shards(): lax.all_to_all(scored.reshape(SLOTS * 8, 4, LANES), ('grp', 'mem'), split...  9.75 us
    all_to_all x1, starting transfers between devices, shards(): lax.all_to_all(scored.reshape(SLOTS * 8, 4, LANES), ('grp', 'mem'), split...  8.61 us
    all_to_all x1, starting transfers between devices, shards(): lax.all_to_all(outbound, 'grp', split_axis=0, concat_axis=0, tiled=True)  7.58 us
    all_to_all x1, waiting for transfers between devices, shards(): lax.all_to_all(outbound, 'grp', split_axis=0, concat_axis=0, tiled=True)  6.27 us
    unnamed x19, local copies, waits for them, and re-layouts  3 us
    pallas_call x1, Pallas kernels, pack(): pl.pallas_call(pack_kernel, out_shape=jax.ShapeDtypeStruct((SLOTS, ROWS,...  1.52 us
  transfers between devices with their start and end apart: 2, of which 2 were waited for; matrix products, arithmetic and copies ran while one was open for 5% of the time, Pallas kernels for 0%

profile of v2, /device:TPU:1, one launch (start us, length us, event | category | flops | bytes accessed | tf_op | source)
XLA Modules:
  0.0 75.2 jit_solution(18144138723505538733)
XLA Ops:
  0.6 0.0 copy-start
  0.6 1.0 %copy-done = f32[1,1,8,16000]{3,2,1,0:T(8,128)S(1)} copy-done((f32[1,1,8,16000]{3,2,1,0:T(8,128)S(1)}, f32[1,1,8,16000]{3,2,1,0:T(8,128)}, u32[]{:S(2)}) %copy-start) | copy-done | bytes 512024
  1.7 0.0 copy-start.1
  1.7 0.7 copy-done.1
  2.3 0.0 copy-start.7
  2.3 1.5 %pack.1 = bf16[16,128,128]{2,1,0:T(8,128)(2,1)} custom-call(s32[8]{0:T(128)S(1)} %bitcast.15, f32[1000,128]{1,0:T(8,128)S(1)} %bitcast.14), custom_call_target="tpu_custom_call" | custom-call | tf_op jit(solution)/shard_map/pack/pallas_call | solution.py:63
  3.8 7.6 %all-to-all-start = ((bf16[16,128,128]{2,1,0:T(8,128)(2,1)}), bf16[16,128,128]{2,1,0:T(8,128)(2,1)S(1)}, u32[]{:S(2)}, u32[]{:S(2)}) async-start(bf16[16,128,128]{2,1,0:T(8,128)(2,1)} %pack.1), calls=%async_computation | async-start | bytes 1048576 | tf_op jit(solution)/shard_map/all_to_all | solution.py:444
  11.4 0.0 copy-done.7
  11.4 0.0 copy-start.8
  11.5 1.3 %copy.14 = bf16[1,2048,192]{2,1,0:T(8,128)(2,1)} copy(bf16[1,2048,192]{1,2,0:T(8,128)(2,1)S(1)} %copy-done.7) | data formatting | bytes 1572864 | tf_op args[10]
  12.7 0.0 copy-done.6
  12.8 0.0 copy-start.5
  12.8 1.2 %pad.12.front_h = bf16[624,1024]{1,0:T(8,128)(2,1)} pad(bf16[400,1024]{1,0:T(8,128)(2,1)S(1)} %copy-done.6, bf16[]{:T(256)} %constant.6.clone.1), padding=112_112x0_0 | pad | bytes 2097154 | tf_op jit(solution)/shard_map/jit(_pad)/pad | solution.py:422
  14.0 0.0 copy-done.8
  14.0 1.5 %fusion.2.pair_h = bf16[7,512,256]{2,1,0:T(8,128)(2,1)} fusion(bf16[7,384,128]{2,1,0:T(8,128)(2,1)S(1)} %copy-done.8), kind=kLoop, calls=%fused_computation.4 | loop fusion | flops 7340032 | bytes 2523136 | tf_op jit(solution)/shard_map/concatenate | solution.py:425
  15.5 6.3 %all-to-all-done.recv_ref = bf16[16,128,128]{2,1,0:T(8,128)(2,1)S(1)} async-done(((bf16[16,128,128]{2,1,0:T(8,128)(2,1)}), bf16[16,128,128]{2,1,0:T(8,128)(2,1)S(1)}, u32[]{:S(2)}, u32[]{:S(2)}) %all-to-all-start) | async-done | bytes 524320 | tf_op jit(solution)/shard_map/all_to_all | solution.py:444
  21.7 0.0 copy-done.2
  21.7 0.0 copy-done.3
  21.7 0.0 copy-done.4
  21.8 0.0 copy-done.5
  21.8 34.0 %family.1 = bf16[512,128]{1,0:T(8,128)(2,1)} custom-call(bf16[16,128,128]{2,1,0:T(8,128)(2,1)S(1)} %all-to-all-done.recv_ref, bf16[624,1024]{1,0:T(8,128)(2,1)} %pad.12.front_h, bf16[1024,1024]{1,0:T(8,128)(2,1)} %expand_h.1, bf16[7,512,256]{2,1,0:T(8,128)(2,1)} %fusion.2.pair_h, bf16[1024,1024]{1,0:T(8,128)(2,1)} %merge_h.1, ...), custom_call_target="tpu_custom_call" | custom-call | flops 20000000000 | bytes 10000000 | tf_op jit(solution)/shard_map/family/pallas_call | solution.py:347
  55.8 8.6 %all-to-all-start.1 = ((bf16[128,4,128]{2,1,0:T(4,128)(2,1)}), bf16[128,4,128]{2,1,0:T(4,128)(2,1)S(1)}, u32[]{:S(2)}, u32[]{:S(2)}) async-start(bf16[128,4,128]{2,1,0:T(4,128)(2,1)} %bitcast.9), calls=%async_computation.1 | async-start | bytes 262144 | tf_op jit(solution)/shard_map/all_to_all | solution.py:461
  64.4 9.7 %all-to-all-done.1 = bf16[128,4,128]{2,1,0:T(4,128)(2,1)S(1)} async-done(((bf16[128,4,128]{2,1,0:T(4,128)(2,1)}), bf16[128,4,128]{2,1,0:T(4,128)(2,1)S(1)}, u32[]{:S(2)}, u32[]{:S(2)}) %all-to-all-start.1) | async-done | bytes 131104 | tf_op jit(solution)/shard_map/all_to_all | solution.py:461
  74.1 1.0 %home.1 = (f32[1,8,107]{2,1,0:T(8,128)}, f32[1,8,64]{2,1,0:T(8,128)}) custom-call(s32[1]{0:T(128)} %bitcast.mem_ref, bf16[512,128]{1,0:T(8,128)(2,1)S(1)} %bitcast.13), custom_call_target="tpu_custom_call" | custom-call | tf_op jit(solution)/shard_map/home/pallas_call | solution.py:404
  (4 shorter events, 0.0 us)
Async XLA Ops:
  0.6 1.0 %copy-start = (f32[1,1,8,16000]{3,2,1,0:T(8,128)S(1)}, f32[1,1,8,16000]{3,2,1,0:T(8,128)}, u32[]{:S(2)}) copy-start(f32[1,1,8,16000]{3,2,1,0:T(8,128)} %param.12) | copy-start | bytes 1536004
  1.7 0.7 copy-start.1
  2.3 9.1 %copy-start.7 = (bf16[1,2048,192]{1,2,0:T(8,128)(2,1)S(1)}, bf16[1,2048,192]{1,2,0:T(8,128)(2,1)}, u32[]{:S(2)}) copy-start(bf16[1,2048,192]{1,2,0:T(8,128)(2,1)} %param.22) | copy-start | bytes 2359300
  2.3 10.4 %copy-start.6 = (bf16[400,1024]{1,0:T(8,128)(2,1)S(1)}, bf16[400,1024]{1,0:T(8,128)(2,1)}, u32[]{:S(2)}) copy-start(bf16[400,1024]{1,0:T(8,128)(2,1)} %param.14) | copy-start | bytes 2457604
  3.8 17.9 %all-to-all-start = ((bf16[16,128,128]{2,1,0:T(8,128)(2,1)}), bf16[16,128,128]{2,1,0:T(8,128)(2,1)S(1)}, u32[]{:S(2)}, u32[]{:S(2)}) async-start(bf16[16,128,128]{2,1,0:T(8,128)(2,1)} %pack.1), calls=%async_computation | async-start | bytes 1048576 | tf_op jit(solution)/shard_map/all_to_all | solution.py:444
  11.4 2.6 %copy-start.8 = (bf16[7,384,128]{2,1,0:T(8,128)(2,1)S(1)}, bf16[7,384,128]{2,1,0:T(8,128)(2,1)}, u32[]{:S(2)}) copy-start(bf16[7,384,128]{2,1,0:T(8,128)(2,1)} %param.16) | copy-start | bytes 2064388
  12.8 9.0 %copy-start.2 = (bf16[1024,128]{1,0:T(8,128)(2,1)S(1)}, bf16[1024,128]{1,0:T(8,128)(2,1)}, u32[]{:S(2)}) copy-start(bf16[1024,128]{1,0:T(8,128)(2,1)} %squeeze_h.1) | copy-start | bytes 786436
  12.8 9.0 %copy-start.3 = (bf16[128,1024]{1,0:T(8,128)(2,1)S(1)}, bf16[128,1024]{1,0:T(8,128)(2,1)}, u32[]{:S(2)}) copy-start(bf16[128,1024]{1,0:T(8,128)(2,1)} %excite_h.1) | copy-start | bytes 786436
  12.8 9.0 %copy-start.4 = (bf16[1,128,1024]{2,1,0:T(8,128)(2,1)S(1)}, bf16[1,128,1024]{2,1,0:T(8,128)(2,1)}, u32[]{:S(2)}) copy-start(bf16[1,128,1024]{2,1,0:T(8,128)(2,1)} %param.21) | copy-start | bytes 786436
  12.8 9.0 %copy-start.5 = (bf16[1,192,107]{2,1,0:T(8,128)(2,1)S(1)}, bf16[1,192,107]{2,1,0:T(8,128)(2,1)}, u32[]{:S(2)}) copy-start(bf16[1,192,107]{2,1,0:T(8,128)(2,1)} %param.23) | copy-start | bytes 123268
  55.8 18.4 %all-to-all-start.1 = ((bf16[128,4,128]{2,1,0:T(4,128)(2,1)}), bf16[128,4,128]{2,1,0:T(4,128)(2,1)S(1)}, u32[]{:S(2)}, u32[]{:S(2)}) async-start(bf16[128,4,128]{2,1,0:T(4,128)(2,1)} %bitcast.9), calls=%async_computation.1 | async-start | bytes 262144 | tf_op jit(solution)/shard_map/all_to_all | solution.py:461

commit v3 on v2

--- a/solution.py
+++ b/solution.py
@@ -32,6 +32,8 @@
 EPS_STAT = 1e-05
 EPS_NORM = 1e-06
 
+LOG2E = 1.4426950408889634
+
 F32 = jnp.float32
 BF16 = jnp.bfloat16
 
@@ -50,13 +52,25 @@
     return out[:rows] + (out[rows : 2 * rows] + out[2 * rows :])
 
 
-def pack_kernel(dest_ref, bank_ref, out_ref, row_ref):
+def pack_kernel(dest_ref, bank_ref, out_ref, held, rows, sems):
+    part = ROWS // 4
+    copies = []
+    for c in range(4):
+        span = pl.ds(c * part * STORE, (min(FLAT, (c + 1) * part) - c * part) * STORE)
+        copies.append(pltpu.make_async_copy(bank_ref.at[span], held.at[span], sems.at[c]))
+    for copy in copies:
+        copy.start()
     out_ref[...] = jnp.zeros_like(out_ref)
-    row_ref[FLAT:] = jnp.zeros((ROWS - FLAT, LANES), F32)
-    for s in range(STORE):
-        row_ref[:FLAT] = bank_ref[pl.ds(s, FLAT, stride=STORE), :]
-        row_ref[FLAT:] = jnp.full((ROWS - FLAT, LANES), s + 1, F32)
-        out_ref[dest_ref[s]] = row_ref[...].astype(BF16)
+    for c in range(4):
+        copies[c].wait()
+        filled = min(FLAT, (c + 1) * part) - c * part
+        for s in range(STORE):
+            values = held[pl.ds(c * part * STORE + s, filled, stride=STORE), :]
+            if filled < part:
+                rows[s, :filled] = values
+                rows[s, filled:] = jnp.full((part - filled, LANES), s + 1, F32)
+                values = rows[s]
+            out_ref[dest_ref[s], c * part : (c + 1) * part] = values.astype(BF16)
 
 
 def pack(bank, dest):
@@ -65,11 +79,15 @@
         out_shape=jax.ShapeDtypeStruct((SLOTS, ROWS, LANES), BF16),
         in_specs=[
             pl.BlockSpec(memory_space=pltpu.SMEM),
-            pl.BlockSpec(memory_space=pltpu.VMEM),
+            pl.BlockSpec(memory_space=pl.ANY),
         ],
         out_specs=pl.BlockSpec(memory_space=pltpu.VMEM),
-        scratch_shapes=[pltpu.VMEM((ROWS, LANES), F32)],
-        compiler_params=pltpu.CompilerParams(vmem_limit_bytes=16 << 20),
+        scratch_shapes=[
+            pltpu.VMEM((FLAT * STORE, LANES), F32),
+            pltpu.VMEM((STORE, ROWS // 4, LANES), F32),
+            pltpu.SemaphoreType.DMA((4,)),
+        ],
+        compiler_params=pltpu.CompilerParams(vmem_limit_bytes=60 << 20),
         name="pack",
     )(dest, bank)
 
@@ -133,7 +151,8 @@
     first,
     second,
 ):
-    mb = 40
+    wb = 512
+    eb, tb, pb = 40, 20, 20
     nb = 256
     copies = [
         pltpu.make_async_copy(source, target, sems.at[i])
@@ -169,8 +188,8 @@
     nk = nb // LANES
 
     def front_cols(n, carry):
-        cols = pl.ds(pl.multiple_of(n * nb, nb), nb)
-        blocks = [n * nk + k for k in range(nk)]
+        cols = pl.ds(pl.multiple_of(n * wb, wb), wb)
+        blocks = [n * (wb // LANES) + k for k in range(wb // LANES)]
         for j in range(SUPER):
             start = MELS * (j - 2)
             block, offset = start // LANES, start % LANES
@@ -184,14 +203,14 @@
             top = PAD_TOP - offset
             out = dot(window, front_w[top : top + 4 * LANES, cols])
             if j == 0:
-                sample = jnp.maximum(out, 0.0).reshape(NSUPER, SLOTS, nb)
+                sample = jnp.maximum(out, 0.0).reshape(NSUPER, SLOTS, wb)
                 first[:, cols] = jnp.sum(sample, axis=0) * (1.0 / NSUPER)
-            out = jnp.maximum(out.astype(BF16), 0.0).reshape(NSUPER, SLOTS, nb)
+            out = jnp.maximum(out.astype(BF16), 0.0).reshape(NSUPER, SLOTS, wb)
             for i, k in enumerate(blocks):
                 front[:, j, k] = out[:, :, i * LANES : (i + 1) * LANES]
         return carry
 
-    lax.fori_loop(0, CH // nb, front_cols, 0)
+    lax.fori_loop(0, CH // wb, front_cols, 0)
 
     nf = CH // LANES
     frames = front.reshape(FRAMES, nf, SLOTS, LANES)
@@ -201,19 +220,18 @@
     wide[0:2] = edge
     wide[FRAMES + 2 : FRAMES + 4] = edge
 
-    def expand_rows(c, carry):
-        f0 = c * mb
-        rows = get(frames, pl.ds(f0, mb), range(nf)).reshape(mb * SLOTS, CH)
+    def expand_rows(f0):
+        rows = get(frames, slice(f0, f0 + eb), range(nf)).reshape(eb * SLOTS, CH)
         for n in range(CH // nb):
             cols = slice(n * nb, (n + 1) * nb)
             out = jnp.maximum(dot(rows, expand_w[:, cols]).astype(BF16), 0.0)
-            out = out.reshape(mb, SLOTS, nb)
-            put(wide, pl.ds(f0 + 2, mb), range(n * nk, (n + 1) * nk), out)
+            out = out.reshape(eb, SLOTS, nb)
+            put(wide, slice(f0 + 2, f0 + 2 + eb), range(n * nk, (n + 1) * nk), out)
             if n == 0:
-                joined[pl.ds(f0, mb), 0] = out[:, :, :BR]
-        return carry
-
-    lax.fori_loop(0, FRAMES // mb, expand_rows, 0)
+                joined[slice(f0, f0 + eb), 0] = out[:, :, :BR]
+
+    for f0 in range(0, FRAMES, eb):
+        expand_rows(f0)
 
     copies[2].wait()
     nq = FRAMES // 4
@@ -251,17 +269,16 @@
     copies[3].wait()
     total[...] = jnp.zeros_like(total)
 
-    def merge_rows(c, carry):
-        f0 = c * mb
-        rows = get(joined, pl.ds(f0, mb), range(nf)).reshape(mb * SLOTS, CH)
+    def merge_rows(f0):
+        rows = get(joined, slice(f0, f0 + eb), range(nf)).reshape(eb * SLOTS, CH)
         for n in range(CH // nb):
             cols = slice(n * nb, (n + 1) * nb)
-            out = jnp.maximum(dot(rows, merge_w[:, cols]), 0.0).reshape(mb, SLOTS, nb)
-            put(merged, pl.ds(f0, mb), range(n * nk, (n + 1) * nk), out.astype(BF16))
+            out = jnp.maximum(dot(rows, merge_w[:, cols]), 0.0).reshape(eb, SLOTS, nb)
+            put(merged, slice(f0, f0 + eb), range(n * nk, (n + 1) * nk), out.astype(BF16))
             total[:, cols] += jnp.sum(out, axis=0)
-        return carry
-
-    lax.fori_loop(0, FRAMES // mb, merge_rows, 0)
+
+    for f0 in range(0, FRAMES, eb):
+        merge_rows(f0)
 
     for k in range(4, 10):
         copies[k].wait()
@@ -274,31 +291,30 @@
     first[...] = jnp.zeros_like(first)
     second[...] = jnp.zeros_like(second)
 
-    def trunk_rows(c, carry):
-        f0 = c * mb
-        acc = jnp.zeros((mb * SLOTS, ATT), F32)
+    def trunk_rows(f0):
+        acc = jnp.zeros((tb * SLOTS, ATT), F32)
         for n in range(CH // nb):
             cols = slice(n * nb, (n + 1) * nb)
             blocks = range(n * nk, (n + 1) * nk)
-            out = get(frames, pl.ds(f0, mb), blocks) + (
-                get(merged, pl.ds(f0, mb), blocks) * gate[:, cols][None]
+            out = get(frames, slice(f0, f0 + tb), blocks) + (
+                get(merged, slice(f0, f0 + tb), blocks) * gate[:, cols][None]
             )
-            put(frames, pl.ds(f0, mb), blocks, out)
+            put(frames, slice(f0, f0 + tb), blocks, out)
             off = out - shift[:, cols][None]
             first[:, cols] += slot_sums(fours(off))
             second[:, cols] += slot_sums(fours(off * off))
-            acc = acc + dot(out.reshape(mb * SLOTS, nb), attend_w[cols, :])
-        pre[pl.ds(f0, mb)] = acc.reshape(mb, SLOTS, ATT)
-        return carry
-
-    lax.fori_loop(0, FRAMES // mb, trunk_rows, 0)
+            acc = acc + dot(out.reshape(tb * SLOTS, nb), attend_w[cols, :])
+        pre[slice(f0, f0 + tb)] = acc.reshape(tb, SLOTS, ATT)
+
+    for f0 in range(0, FRAMES, tb):
+        trunk_rows(f0)
 
     drift = first[...] * (1.0 / FRAMES)
     center = shift.astype(F32) + drift
     variance = jnp.maximum(second[...] * (1.0 / FRAMES) - drift * drift, 0.0)
     spread = jnp.sqrt(variance + EPS_STAT)
     context = exact_dot(center, attend_w[CH : 2 * CH]) + exact_dot(spread, attend_w[2 * CH :])
-    attended[...] = jnp.tanh(pre[...] + context[None]).astype(BF16)
+    attended[...] = (jnp.tanh(pre[...] + context[None]) * LOG2E).astype(BF16)
 
     first[...] = center
     second[...] = 1.0 / spread
@@ -309,11 +325,11 @@
         middle = first[:, cols].astype(BF16)
         scale = second[:, cols].astype(BF16)
         parts = []
-        for f0 in range(0, FRAMES, mb):
-            rows = attended[f0 : f0 + mb].reshape(mb * SLOTS, ATT)
-            energy = dot(rows, score_w[:, cols]).reshape(mb, SLOTS, nb)
-            weight = jnp.exp(energy).astype(BF16)
-            z = (get(frames, slice(f0, f0 + mb), blocks) - middle[None]) * scale[None]
+        for f0 in range(0, FRAMES, pb):
+            rows = attended[f0 : f0 + pb].reshape(pb * SLOTS, ATT)
+            energy = dot(rows, score_w[:, cols]).reshape(pb, SLOTS, nb)
+            weight = jnp.exp2(energy).astype(BF16)
+            z = (get(frames, slice(f0, f0 + pb), blocks) - middle[None]) * scale[None]
             wz = weight * z
             parts.append((fours(weight), fours(wz), fours(wz * z)))
         s0, s1, s2 = (slot_sums(jnp.concatenate(part, axis=0)) for part in zip(*parts))
@@ -439,7 +455,8 @@
     embed_weight,
     language_weight,
 ):
-    bank = filterbank.reshape(STORE, FLAT, LANES).transpose(1, 0, 2).reshape(FLAT * STORE, LANES)
+    bank = filterbank.reshape(STORE, FLAT, LANES).transpose(1, 0, 2)
+    bank = bank.reshape(FLAT * STORE, LANES)
     outbound = pack(bank, destination.reshape(STORE))
     arrived = lax.all_to_all(outbound, "grp", split_axis=0, concat_axis=0, tiled=True)
     tall, pairs = prepare(initial_conv_weight, branch_weight)

time: 75.5 us -> 72.8 us (0.964)
  local copies, waits for them, and re-layouts: 4.23 us -> 2.55 us
  Pallas kernels: 36.5 us -> 35.6 us
    pallas_call x1, Pallas kernels: 34 us -> 31.8 us  [family(): pl.pallas_call(family_kernel, out_shape=jax.ShapeDtypeStruct((SLOTS * 8 *...]
    unnamed x19 -> x15, local copies, waits for them, and re-layouts: 3 us -> 1.32 us
    pallas_call x1, Pallas kernels: 1.52 us -> 2.77 us  [pack(): pl.pallas_call(pack_kernel, out_shape=jax.ShapeDtypeStruct((SLOTS, ROWS,...]
where the time goes in v3:
time: 72.8 us; the launch traced here: 72.5 us
  Pallas kernels  35.6 us (49%)
  starting transfers between devices  16.2 us (22%)
  waiting for transfers between devices  16 us (22%)
  local copies, waits for them, and re-layouts  2.55 us (4%)
  other arithmetic  1.47 us (2%)
  between operations  0.73 us (1%)
    pallas_call x1, Pallas kernels, family(): pl.pallas_call(family_kernel, out_shape=jax.ShapeDtypeStruct((SLOTS * 8 *...  31.8 us
    all_to_all x1, waiting for transfers between devices, shards(): lax.all_to_all(scored.reshape(SLOTS * 8, 4, LANES), ('grp', 'mem'), split...  9.75 us
    all_to_all x1, starting transfers between devices, shards(): lax.all_to_all(scored.reshape(SLOTS * 8, 4, LANES), ('grp', 'mem'), split...  8.6 us
    all_to_all x1, starting transfers between devices, shards(): lax.all_to_all(outbound, 'grp', split_axis=0, concat_axis=0, tiled=True)  7.6 us
    all_to_all x1, waiting for transfers between devices, shards(): lax.all_to_all(outbound, 'grp', split_axis=0, concat_axis=0, tiled=True)  6.26 us
    pallas_call x1, Pallas kernels, pack(): pl.pallas_call(pack_kernel, out_shape=jax.ShapeDtypeStruct((SLOTS, ROWS,...  2.77 us
    concatenate x1, other arithmetic, prepare(): return (tall, jnp.concatenate([early, late], axis=2))  1.47 us
  transfers between devices with their start and end apart: 2, of which 2 were waited for; matrix products, arithmetic and copies ran while one was open for 5% of the time, Pallas kernels for 0%

profile of v3, /device:TPU:1, one launch (start us, length us, event | category | flops | bytes accessed | tf_op | source)
XLA Modules:
  0.0 72.5 jit_solution(14856539699634526343)
XLA Ops:
  0.6 0.0 copy-start.5
  0.6 0.0 copy-start.4
  0.7 2.8 %pack.1 = bf16[16,128,128]{2,1,0:T(8,128)(2,1)} custom-call(s32[8]{0:T(128)} %bitcast.18, f32[1000,128]{1,0:T(8,128)} %bitcast.17), custom_call_target="tpu_custom_call" | custom-call | tf_op jit(solution)/shard_map/pack/pallas_call | solution.py:77
  3.4 7.6 %all-to-all-start = ((bf16[16,128,128]{2,1,0:T(8,128)(2,1)}), bf16[16,128,128]{2,1,0:T(8,128)(2,1)S(1)}, u32[]{:S(2)}, u32[]{:S(2)}) async-start(bf16[16,128,128]{2,1,0:T(8,128)(2,1)} %pack.1), calls=%async_computation | async-start | bytes 1048576 | tf_op jit(solution)/shard_map/all_to_all | solution.py:461
  11.0 0.0 copy-done.5
  11.0 0.0 copy-start.6
  11.1 1.3 %copy.14 = bf16[1,2048,192]{2,1,0:T(8,128)(2,1)} copy(bf16[1,2048,192]{1,2,0:T(8,128)(2,1)S(1)} %copy-done.5) | data formatting | bytes 1572864 | tf_op args[10]
  12.3 0.0 copy-done.4
  12.4 0.0 copy-start
  12.4 0.0 copy-start.1
  12.4 0.0 copy-start.2
  12.4 0.0 copy-start.3
  12.4 1.2 %pad.12.front_h = bf16[624,1024]{1,0:T(8,128)(2,1)} pad(bf16[400,1024]{1,0:T(8,128)(2,1)S(1)} %copy-done.4, bf16[]{:T(256)} %constant.6.clone.1), padding=112_112x0_0 | pad | bytes 2097154 | tf_op jit(solution)/shard_map/jit(_pad)/pad | solution.py:438
  13.6 0.0 copy-done.6
  13.6 1.5 %fusion.2.pair_h = bf16[7,512,256]{2,1,0:T(8,128)(2,1)} fusion(bf16[7,384,128]{2,1,0:T(8,128)(2,1)S(1)} %copy-done.6), kind=kLoop, calls=%fused_computation.4 | loop fusion | flops 7340032 | bytes 2523136 | tf_op jit(solution)/shard_map/concatenate | solution.py:441
  15.1 6.3 %all-to-all-done.recv_ref = bf16[16,128,128]{2,1,0:T(8,128)(2,1)S(1)} async-done(((bf16[16,128,128]{2,1,0:T(8,128)(2,1)}), bf16[16,128,128]{2,1,0:T(8,128)(2,1)S(1)}, u32[]{:S(2)}, u32[]{:S(2)}) %all-to-all-start) | async-done | bytes 524320 | tf_op jit(solution)/shard_map/all_to_all | solution.py:461
  21.3 0.0 copy-done
  21.3 0.0 copy-done.1
  21.3 0.0 copy-done.2
  21.3 0.0 copy-done.3
  21.4 31.8 %family.1 = bf16[512,128]{1,0:T(8,128)(2,1)} custom-call(bf16[16,128,128]{2,1,0:T(8,128)(2,1)S(1)} %all-to-all-done.recv_ref, bf16[624,1024]{1,0:T(8,128)(2,1)} %pad.12.front_h, bf16[1024,1024]{1,0:T(8,128)(2,1)} %expand_h.1, bf16[7,512,256]{2,1,0:T(8,128)(2,1)} %fusion.2.pair_h, bf16[1024,1024]{1,0:T(8,128)(2,1)} %merge_h.1, bf16[1024,128]{1,0:T(8,128)(2,1)S(1)} %copy-done, ...), custom_call_target="tpu_custom_call" | custom-call | flops 20000000000 | bytes 10000000 | tf_op jit(solution)/shard_map/family/pallas_call | solution.py:363
  53.1 8.6 %all-to-all-start.1 = ((bf16[128,4,128]{2,1,0:T(4,128)(2,1)}), bf16[128,4,128]{2,1,0:T(4,128)(2,1)S(1)}, u32[]{:S(2)}, u32[]{:S(2)}) async-start(bf16[128,4,128]{2,1,0:T(4,128)(2,1)} %bitcast.9), calls=%async_computation.1 | async-start | bytes 262144 | tf_op jit(solution)/shard_map/all_to_all | solution.py:478
  61.7 9.7 %all-to-all-done.1 = bf16[128,4,128]{2,1,0:T(4,128)(2,1)S(1)} async-done(((bf16[128,4,128]{2,1,0:T(4,128)(2,1)}), bf16[128,4,128]{2,1,0:T(4,128)(2,1)S(1)}, u32[]{:S(2)}, u32[]{:S(2)}) %all-to-all-start.1) | async-done | bytes 131104 | tf_op jit(solution)/shard_map/all_to_all | solution.py:478
  71.5 1.0 %home.1 = (f32[1,8,107]{2,1,0:T(8,128)}, f32[1,8,64]{2,1,0:T(8,128)}) custom-call(s32[1]{0:T(128)} %bitcast.mem_ref, bf16[512,128]{1,0:T(8,128)(2,1)S(1)} %bitcast.13), custom_call_target="tpu_custom_call" | custom-call | tf_op jit(solution)/shard_map/home/pallas_call | solution.py:420
Async XLA Ops:
  0.6 10.4 %copy-start.5 = (bf16[1,2048,192]{1,2,0:T(8,128)(2,1)S(1)}, bf16[1,2048,192]{1,2,0:T(8,128)(2,1)}, u32[]{:S(2)}) copy-start(bf16[1,2048,192]{1,2,0:T(8,128)(2,1)} %param.22) | copy-start | bytes 2359300
  0.6 11.7 %copy-start.4 = (bf16[400,1024]{1,0:T(8,128)(2,1)S(1)}, bf16[400,1024]{1,0:T(8,128)(2,1)}, u32[]{:S(2)}) copy-start(bf16[400,1024]{1,0:T(8,128)(2,1)} %param.14) | copy-start | bytes 2457604
  3.4 17.9 %all-to-all-start = ((bf16[16,128,128]{2,1,0:T(8,128)(2,1)}), bf16[16,128,128]{2,1,0:T(8,128)(2,1)S(1)}, u32[]{:S(2)}, u32[]{:S(2)}) async-start(bf16[16,128,128]{2,1,0:T(8,128)(2,1)} %pack.1), calls=%async_computation | async-start | bytes 1048576 | tf_op jit(solution)/shard_map/all_to_all | solution.py:461
  11.0 2.6 %copy-start.6 = (bf16[7,384,128]{2,1,0:T(8,128)(2,1)S(1)}, bf16[7,384,128]{2,1,0:T(8,128)(2,1)}, u32[]{:S(2)}) copy-start(bf16[7,384,128]{2,1,0:T(8,128)(2,1)} %param.16) | copy-start | bytes 2064388
  12.4 9.0 %copy-start = (bf16[1024,128]{1,0:T(8,128)(2,1)S(1)}, bf16[1024,128]{1,0:T(8,128)(2,1)}, u32[]{:S(2)}) copy-start(bf16[1024,128]{1,0:T(8,128)(2,1)} %squeeze_h.1) | copy-start | bytes 786436
  12.4 9.0 %copy-start.1 = (bf16[128,1024]{1,0:T(8,128)(2,1)S(1)}, bf16[128,1024]{1,0:T(8,128)(2,1)}, u32[]{:S(2)}) copy-start(bf16[128,1024]{1,0:T(8,128)(2,1)} %excite_h.1) | copy-start | bytes 786436
  12.4 9.0 %copy-start.2 = (bf16[1,128,1024]{2,1,0:T(8,128)(2,1)S(1)}, bf16[1,128,1024]{2,1,0:T(8,128)(2,1)}, u32[]{:S(2)}) copy-start(bf16[1,128,1024]{2,1,0:T(8,128)(2,1)} %param.21) | copy-start | bytes 786436
  12.4 9.0 %copy-start.3 = (bf16[1,192,107]{2,1,0:T(8,128)(2,1)S(1)}, bf16[1,192,107]{2,1,0:T(8,128)(2,1)}, u32[]{:S(2)}) copy-start(bf16[1,192,107]{2,1,0:T(8,128)(2,1)} %param.23) | copy-start | bytes 123268
  53.1 18.4 %all-to-all-start.1 = ((bf16[128,4,128]{2,1,0:T(4,128)(2,1)}), bf16[128,4,128]{2,1,0:T(4,128)(2,1)S(1)}, u32[]{:S(2)}, u32[]{:S(2)}) async-start(bf16[128,4,128]{2,1,0:T(4,128)(2,1)} %bitcast.9), calls=%async_computation.1 | async-start | bytes 262144 | tf_op jit(solution)/shard_map/all_to_all | solution.py:478

commit v4 on v3

--- a/solution.py
+++ b/solution.py
@@ -52,25 +52,12 @@
     return out[:rows] + (out[rows : 2 * rows] + out[2 * rows :])
 
 
-def pack_kernel(dest_ref, bank_ref, out_ref, held, rows, sems):
-    part = ROWS // 4
-    copies = []
-    for c in range(4):
-        span = pl.ds(c * part * STORE, (min(FLAT, (c + 1) * part) - c * part) * STORE)
-        copies.append(pltpu.make_async_copy(bank_ref.at[span], held.at[span], sems.at[c]))
-    for copy in copies:
-        copy.start()
+def pack_kernel(dest_ref, bank_ref, out_ref, row_ref):
     out_ref[...] = jnp.zeros_like(out_ref)
-    for c in range(4):
-        copies[c].wait()
-        filled = min(FLAT, (c + 1) * part) - c * part
-        for s in range(STORE):
-            values = held[pl.ds(c * part * STORE + s, filled, stride=STORE), :]
-            if filled < part:
-                rows[s, :filled] = values
-                rows[s, filled:] = jnp.full((part - filled, LANES), s + 1, F32)
-                values = rows[s]
-            out_ref[dest_ref[s], c * part : (c + 1) * part] = values.astype(BF16)
+    for s in range(STORE):
+        row_ref[:FLAT] = bank_ref[pl.ds(s, FLAT, stride=STORE), :]
+        row_ref[FLAT:] = jnp.full((ROWS - FLAT, LANES), s + 1, F32)
+        out_ref[dest_ref[s]] = row_ref[...].astype(BF16)
 
 
 def pack(bank, dest):
@@ -79,15 +66,10 @@
         out_shape=jax.ShapeDtypeStruct((SLOTS, ROWS, LANES), BF16),
         in_specs=[
             pl.BlockSpec(memory_space=pltpu.SMEM),
-            pl.BlockSpec(memory_space=pl.ANY),
+            pl.BlockSpec(memory_space=pltpu.VMEM),
         ],
         out_specs=pl.BlockSpec(memory_space=pltpu.VMEM),
-        scratch_shapes=[
-            pltpu.VMEM((FLAT * STORE, LANES), F32),
-            pltpu.VMEM((STORE, ROWS // 4, LANES), F32),
-            pltpu.SemaphoreType.DMA((4,)),
-        ],
-        compiler_params=pltpu.CompilerParams(vmem_limit_bytes=60 << 20),
+        scratch_shapes=[pltpu.VMEM((ROWS, LANES), F32)],
         name="pack",
     )(dest, bank)
 
@@ -171,8 +153,7 @@
             ]
         )
     ]
-    for copy in copies:
-        copy.start()
+    copies[0].start()
 
     for s in range(SLOTS):
         flat[pl.ds(s, ROWS, stride=SLOTS), :] = recv_ref[s].astype(F32)
@@ -184,6 +165,8 @@
     )
 
     copies[0].wait()
+    for copy in copies[1:]:
+        copy.start()
 
     nk = nb // LANES
 
@@ -205,7 +188,7 @@
             if j == 0:
                 sample = jnp.maximum(out, 0.0).reshape(NSUPER, SLOTS, wb)
                 first[:, cols] = jnp.sum(sample, axis=0) * (1.0 / NSUPER)
-            out = jnp.maximum(out.astype(BF16), 0.0).reshape(NSUPER, SLOTS, wb)
+            out = jnp.maximum(out, 0.0).astype(BF16).reshape(NSUPER, SLOTS, wb)
             for i, k in enumerate(blocks):
                 front[:, j, k] = out[:, :, i * LANES : (i + 1) * LANES]
         return carry
@@ -224,7 +207,7 @@
         rows = get(frames, slice(f0, f0 + eb), range(nf)).reshape(eb * SLOTS, CH)
         for n in range(CH // nb):
             cols = slice(n * nb, (n + 1) * nb)
-            out = jnp.maximum(dot(rows, expand_w[:, cols]).astype(BF16), 0.0)
+            out = jnp.maximum(dot(rows, expand_w[:, cols]), 0.0).astype(BF16)
             out = out.reshape(eb, SLOTS, nb)
             put(wide, slice(f0 + 2, f0 + 2 + eb), range(n * nk, (n + 1) * nk), out)
             if n == 0:
@@ -256,7 +239,7 @@
                 ],
                 axis=0,
             ).reshape(2 * n * SLOTS, 4 * BR)
-            out = jnp.maximum(dot(rows, pair_w[i - 1]).astype(BF16), 0.0)
+            out = jnp.maximum(dot(rows, pair_w[i - 1]), 0.0).astype(BF16)
             out = out.reshape(2, n, SLOTS, 2 * BR)
             for p in range(2):
                 early, late = out[p, :, :, :BR], out[p, :, :, BR:]

time: 72.8 us -> 72.3 us (level)
  transfers between devices with their start and end apart: 2 -> 2, of which waited for: 2 -> 2; matrix products, arithmetic and copies ran while one was open for 5% -> 6% of each run, Pallas kernels for 0% -> 0%
where the time goes in v4:
time: 72.3 us; the launch traced here: 72 us
  Pallas kernels  35 us (48%)
  starting transfers between devices  16.2 us (22%)
  waiting for transfers between devices  16 us (22%)
  local copies, waits for them, and re-layouts  2.55 us (4%)
  other arithmetic  1.47 us (2%)
    pallas_call x1, Pallas kernels, family(): pl.pallas_call(family_kernel, out_shape=jax.ShapeDtypeStruct((SLOTS * 8 *...  31.8 us
    all_to_all x1, waiting for transfers between devices, shards(): lax.all_to_all(scored.reshape(SLOTS * 8, 4, LANES), ('grp', 'mem'), split...  9.75 us
    all_to_all x1, starting transfers between devices, shards(): lax.all_to_all(scored.reshape(SLOTS * 8, 4, LANES), ('grp', 'mem'), split...  8.6 us
    all_to_all x1, starting transfers between devices, shards(): lax.all_to_all(outbound, 'grp', split_axis=0, concat_axis=0, tiled=True)  7.58 us
    all_to_all x1, waiting for transfers between devices, shards(): lax.all_to_all(outbound, 'grp', split_axis=0, concat_axis=0, tiled=True)  6.26 us
    pallas_call x1, Pallas kernels, pack(): pl.pallas_call(pack_kernel, out_shape=jax.ShapeDtypeStruct((SLOTS, ROWS,...  2.15 us
    concatenate x1, other arithmetic, prepare(): return (tall, jnp.concatenate([early, late], axis=2))  1.47 us
  transfers between devices with their start and end apart: 2, of which 2 were waited for; matrix products, arithmetic and copies ran while one was open for 6% of the time, Pallas kernels for 0%

profile of v4, /device:TPU:1, one launch (start us, length us, event | category | flops | bytes accessed | tf_op | source)
XLA Modules:
  0.0 72.0 jit_solution(12865544793185106148)
XLA Ops:
  0.6 0.0 copy-start.5
  0.6 0.0 copy-start.4
  0.7 2.1 %pack.1 = bf16[16,128,128]{2,1,0:T(8,128)(2,1)} custom-call(s32[8]{0:T(128)} %bitcast.18, f32[1000,128]{1,0:T(8,128)} %bitcast.17), custom_call_target="tpu_custom_call" | custom-call | tf_op jit(solution)/shard_map/pack/pallas_call | solution.py:64
  2.8 7.6 %all-to-all-start = ((bf16[16,128,128]{2,1,0:T(8,128)(2,1)}), bf16[16,128,128]{2,1,0:T(8,128)(2,1)S(1)}, u32[]{:S(2)}, u32[]{:S(2)}) async-start(bf16[16,128,128]{2,1,0:T(8,128)(2,1)} %pack.1), calls=%async_computation | async-start | bytes 1048576 | tf_op jit(solution)/shard_map/all_to_all | solution.py:444
  10.4 0.0 copy-done.5
  10.4 0.0 copy-start.6
  10.4 1.3 %copy.14 = bf16[1,2048,192]{2,1,0:T(8,128)(2,1)} copy(bf16[1,2048,192]{1,2,0:T(8,128)(2,1)S(1)} %copy-done.5) | data formatting | bytes 1572864 | tf_op args[10]
  11.7 0.0 copy-done.4
  11.7 0.0 copy-start
  11.7 0.0 copy-start.1
  11.7 0.0 copy-start.2
  11.7 0.0 copy-start.3
  11.7 1.2 %pad.12.front_h = bf16[624,1024]{1,0:T(8,128)(2,1)} pad(bf16[400,1024]{1,0:T(8,128)(2,1)S(1)} %copy-done.4, bf16[]{:T(256)} %constant.6.clone.1), padding=112_112x0_0 | pad | bytes 2097154 | tf_op jit(solution)/shard_map/jit(_pad)/pad | solution.py:421
  13.0 0.0 copy-done.6
  13.0 1.5 %fusion.2.pair_h = bf16[7,512,256]{2,1,0:T(8,128)(2,1)} fusion(bf16[7,384,128]{2,1,0:T(8,128)(2,1)S(1)} %copy-done.6), kind=kLoop, calls=%fused_computation.4 | loop fusion | flops 7340032 | bytes 2523136 | tf_op jit(solution)/shard_map/concatenate | solution.py:424
  14.4 6.3 %all-to-all-done.recv_ref = bf16[16,128,128]{2,1,0:T(8,128)(2,1)S(1)} async-done(((bf16[16,128,128]{2,1,0:T(8,128)(2,1)}), bf16[16,128,128]{2,1,0:T(8,128)(2,1)S(1)}, u32[]{:S(2)}, u32[]{:S(2)}) %all-to-all-start) | async-done | bytes 524320 | tf_op jit(solution)/shard_map/all_to_all | solution.py:444
  20.7 0.0 copy-done
  20.7 0.0 copy-done.1
  20.7 0.0 copy-done.2
  20.7 0.0 copy-done.3
  20.7 31.8 %family.1 = bf16[512,128]{1,0:T(8,128)(2,1)} custom-call(bf16[16,128,128]{2,1,0:T(8,128)(2,1)S(1)} %all-to-all-done.recv_ref, bf16[624,1024]{1,0:T(8,128)(2,1)} %pad.12.front_h, bf16[1024,1024]{1,0:T(8,128)(2,1)} %expand_h.1, bf16[7,512,256]{2,1,0:T(8,128)(2,1)} %fusion.2.pair_h, bf16[1024,1024]{1,0:T(8,128)(2,1)} %merge_h.1, bf16[1024,128]{1,0:T(8,128)(2,1)S(1)} %copy-done, ...), custom_call_target="tpu_custom_call" | custom-call | flops 20000000000 | bytes 10000000 | tf_op jit(solution)/shard_map/family/pallas_call | solution.py:346
  52.6 8.6 %all-to-all-start.1 = ((bf16[128,4,128]{2,1,0:T(4,128)(2,1)}), bf16[128,4,128]{2,1,0:T(4,128)(2,1)S(1)}, u32[]{:S(2)}, u32[]{:S(2)}) async-start(bf16[128,4,128]{2,1,0:T(4,128)(2,1)} %bitcast.9), calls=%async_computation.1 | async-start | bytes 262144 | tf_op jit(solution)/shard_map/all_to_all | solution.py:461
  61.2 9.7 %all-to-all-done.1 = bf16[128,4,128]{2,1,0:T(4,128)(2,1)S(1)} async-done(((bf16[128,4,128]{2,1,0:T(4,128)(2,1)}), bf16[128,4,128]{2,1,0:T(4,128)(2,1)S(1)}, u32[]{:S(2)}, u32[]{:S(2)}) %all-to-all-start.1) | async-done | bytes 131104 | tf_op jit(solution)/shard_map/all_to_all | solution.py:461
  70.9 1.0 %home.1 = (f32[1,8,107]{2,1,0:T(8,128)}, f32[1,8,64]{2,1,0:T(8,128)}) custom-call(s32[1]{0:T(128)} %bitcast.mem_ref, bf16[512,128]{1,0:T(8,128)(2,1)S(1)} %bitcast.13), custom_call_target="tpu_custom_call" | custom-call | tf_op jit(solution)/shard_map/home/pallas_call | solution.py:403
Async XLA Ops:
  0.6 9.8 %copy-start.5 = (bf16[1,2048,192]{1,2,0:T(8,128)(2,1)S(1)}, bf16[1,2048,192]{1,2,0:T(8,128)(2,1)}, u32[]{:S(2)}) copy-start(bf16[1,2048,192]{1,2,0:T(8,128)(2,1)} %param.22) | copy-start | bytes 2359300
  0.6 11.1 %copy-start.4 = (bf16[400,1024]{1,0:T(8,128)(2,1)S(1)}, bf16[400,1024]{1,0:T(8,128)(2,1)}, u32[]{:S(2)}) copy-start(bf16[400,1024]{1,0:T(8,128)(2,1)} %param.14) | copy-start | bytes 2457604
  2.8 17.9 %all-to-all-start = ((bf16[16,128,128]{2,1,0:T(8,128)(2,1)}), bf16[16,128,128]{2,1,0:T(8,128)(2,1)S(1)}, u32[]{:S(2)}, u32[]{:S(2)}) async-start(bf16[16,128,128]{2,1,0:T(8,128)(2,1)} %pack.1), calls=%async_computation | async-start | bytes 1048576 | tf_op jit(solution)/shard_map/all_to_all | solution.py:444
  10.4 2.6 %copy-start.6 = (bf16[7,384,128]{2,1,0:T(8,128)(2,1)S(1)}, bf16[7,384,128]{2,1,0:T(8,128)(2,1)}, u32[]{:S(2)}) copy-start(bf16[7,384,128]{2,1,0:T(8,128)(2,1)} %param.16) | copy-start | bytes 2064388
  11.7 9.0 %copy-start = (bf16[1024,128]{1,0:T(8,128)(2,1)S(1)}, bf16[1024,128]{1,0:T(8,128)(2,1)}, u32[]{:S(2)}) copy-start(bf16[1024,128]{1,0:T(8,128)(2,1)} %squeeze_h.1) | copy-start | bytes 786436
  11.7 9.0 %copy-start.1 = (bf16[128,1024]{1,0:T(8,128)(2,1)S(1)}, bf16[128,1024]{1,0:T(8,128)(2,1)}, u32[]{:S(2)}) copy-start(bf16[128,1024]{1,0:T(8,128)(2,1)} %excite_h.1) | copy-start | bytes 786436
  11.7 9.0 %copy-start.2 = (bf16[1,128,1024]{2,1,0:T(8,128)(2,1)S(1)}, bf16[1,128,1024]{2,1,0:T(8,128)(2,1)}, u32[]{:S(2)}) copy-start(bf16[1,128,1024]{2,1,0:T(8,128)(2,1)} %param.21) | copy-start | bytes 786436
  11.7 9.0 %copy-start.3 = (bf16[1,192,107]{2,1,0:T(8,128)(2,1)S(1)}, bf16[1,192,107]{2,1,0:T(8,128)(2,1)}, u32[]{:S(2)}) copy-start(bf16[1,192,107]{2,1,0:T(8,128)(2,1)} %param.23) | copy-start | bytes 123268
  52.6 18.4 %all-to-all-start.1 = ((bf16[128,4,128]{2,1,0:T(4,128)(2,1)}), bf16[128,4,128]{2,1,0:T(4,128)(2,1)S(1)}, u32[]{:S(2)}, u32[]{:S(2)}) async-start(bf16[128,4,128]{2,1,0:T(4,128)(2,1)} %bitcast.9), calls=%async_computation.1 | async-start | bytes 262144 | tf_op jit(solution)/shard_map/all_to_all | solution.py:461

commit v5 on v4

--- a/solution.py
+++ b/solution.py
@@ -313,12 +313,19 @@
             energy = dot(rows, score_w[:, cols]).reshape(pb, SLOTS, nb)
             weight = jnp.exp2(energy).astype(BF16)
             z = (get(frames, slice(f0, f0 + pb), blocks) - middle[None]) * scale[None]
-            wz = weight * z
-            parts.append((fours(weight), fours(wz), fours(wz * z)))
-        s0, s1, s2 = (slot_sums(jnp.concatenate(part, axis=0)) for part in zip(*parts))
+            put(joined, slice(f0, f0 + pb), blocks, weight)
+            parts.append((fours(weight), fours(weight * z)))
+        s0, s1 = (slot_sums(jnp.concatenate(part, axis=0)) for part in zip(*parts))
+        dev = 1.0 / scale.astype(F32)
+        middle = (middle.astype(F32) + s1 / s0 * dev).astype(BF16)
+        parts = []
+        for f0 in range(0, FRAMES, pb):
+            z = (get(frames, slice(f0, f0 + pb), blocks) - middle[None]) * scale[None]
+            wz = get(joined, slice(f0, f0 + pb), blocks) * z
+            parts.append((fours(wz), fours(wz * z)))
+        s1, s2 = (slot_sums(jnp.concatenate(part, axis=0)) for part in zip(*parts))
         m1 = s1 / s0
         m2 = jnp.maximum(s2 / s0 - m1 * m1, 0.0)
-        dev = 1.0 / scale.astype(F32)
         first[:, cols] = middle.astype(F32) + m1 * dev
         second[:, cols] = jnp.sqrt(m2 * dev * dev + EPS_STAT)
     pooled = jnp.concatenate([first[...], second[...]], axis=1).astype(BF16)

time: 72.3 us -> 73.7 us (1.019)
  Pallas kernels: 35 us -> 36.5 us
    pallas_call x1, Pallas kernels: 31.8 us -> 33.3 us  [family(): pl.pallas_call(family_kernel, out_shape=jax.ShapeDtypeStruct((SLOTS * 8 *...]
  transfers between devices with their start and end apart: 2 -> 2, of which waited for: 2 -> 2; matrix products, arithmetic and copies ran while one was open for 6% -> 5% of each run, Pallas kernels for 0% -> 0%
where the time goes in v5:
time: 73.7 us; the launch traced here: 73.4 us
  Pallas kernels  36.5 us (50%)
  starting transfers between devices  16.2 us (22%)
  waiting for transfers between devices  16 us (22%)
  local copies, waits for them, and re-layouts  2.55 us (3%)
  other arithmetic  1.47 us (2%)
    pallas_call x1, Pallas kernels, family(): pl.pallas_call(family_kernel, out_shape=jax.ShapeDtypeStruct((SLOTS * 8 *...  33.3 us
    all_to_all x1, waiting for transfers between devices, shards(): lax.all_to_all(scored.reshape(SLOTS * 8, 4, LANES), ('grp', 'mem'), split...  9.75 us
    all_to_all x1, starting transfers between devices, shards(): lax.all_to_all(scored.reshape(SLOTS * 8, 4, LANES), ('grp', 'mem'), split...  8.59 us
    all_to_all x1, starting transfers between devices, shards(): lax.all_to_all(outbound, 'grp', split_axis=0, concat_axis=0, tiled=True)  7.58 us
    all_to_all x1, waiting for transfers between devices, shards(): lax.all_to_all(outbound, 'grp', split_axis=0, concat_axis=0, tiled=True)  6.26 us
    pallas_call x1, Pallas kernels, pack(): pl.pallas_call(pack_kernel, out_shape=jax.ShapeDtypeStruct((SLOTS, ROWS,...  2.15 us
  transfers between devices with their start and end apart: 2, of which 2 were waited for; matrix products, arithmetic and copies ran while one was open for 5% of the time, Pallas kernels for 0%

profile of v5, /device:TPU:1, one launch (start us, length us, event | category | flops | bytes accessed | tf_op | source)
XLA Modules:
  0.0 73.4 jit_solution(710390733168984826)
XLA Ops:
  0.6 0.0 copy-start.5
  0.6 0.0 copy-start.4
  0.7 2.1 %pack.1 = bf16[16,128,128]{2,1,0:T(8,128)(2,1)} custom-call(s32[8]{0:T(128)} %bitcast.18, f32[1000,128]{1,0:T(8,128)} %bitcast.17), custom_call_target="tpu_custom_call" | custom-call | tf_op jit(solution)/shard_map/pack/pallas_call | solution.py:64
  2.8 7.6 %all-to-all-start = ((bf16[16,128,128]{2,1,0:T(8,128)(2,1)}), bf16[16,128,128]{2,1,0:T(8,128)(2,1)S(1)}, u32[]{:S(2)}, u32[]{:S(2)}) async-start(bf16[16,128,128]{2,1,0:T(8,128)(2,1)} %pack.1), calls=%async_computation | async-start | bytes 1048576 | tf_op jit(solution)/shard_map/all_to_all | solution.py:451
  10.4 0.0 copy-done.5
  10.4 0.0 copy-start.6
  10.4 1.3 %copy.14 = bf16[1,2048,192]{2,1,0:T(8,128)(2,1)} copy(bf16[1,2048,192]{1,2,0:T(8,128)(2,1)S(1)} %copy-done.5) | data formatting | bytes 1572864 | tf_op args[10]
  11.7 0.0 copy-done.4
  11.7 0.0 copy-start
  11.7 0.0 copy-start.1
  11.7 0.0 copy-start.2
  11.7 0.0 copy-start.3
  11.7 1.2 %pad.12.front_h = bf16[624,1024]{1,0:T(8,128)(2,1)} pad(bf16[400,1024]{1,0:T(8,128)(2,1)S(1)} %copy-done.4, bf16[]{:T(256)} %constant.6.clone.1), padding=112_112x0_0 | pad | bytes 2097154 | tf_op jit(solution)/shard_map/jit(_pad)/pad | solution.py:428
  13.0 0.0 copy-done.6
  13.0 1.5 %fusion.2.pair_h = bf16[7,512,256]{2,1,0:T(8,128)(2,1)} fusion(bf16[7,384,128]{2,1,0:T(8,128)(2,1)S(1)} %copy-done.6), kind=kLoop, calls=%fused_computation.4 | loop fusion | flops 7340032 | bytes 2523136 | tf_op jit(solution)/shard_map/concatenate | solution.py:431
  14.4 6.3 %all-to-all-done.recv_ref = bf16[16,128,128]{2,1,0:T(8,128)(2,1)S(1)} async-done(((bf16[16,128,128]{2,1,0:T(8,128)(2,1)}), bf16[16,128,128]{2,1,0:T(8,128)(2,1)S(1)}, u32[]{:S(2)}, u32[]{:S(2)}) %all-to-all-start) | async-done | bytes 524320 | tf_op jit(solution)/shard_map/all_to_all | solution.py:451
  20.7 0.0 copy-done
  20.7 0.0 copy-done.1
  20.7 0.0 copy-done.2
  20.7 0.0 copy-done.3
  20.7 33.3 %family.1 = bf16[512,128]{1,0:T(8,128)(2,1)} custom-call(bf16[16,128,128]{2,1,0:T(8,128)(2,1)S(1)} %all-to-all-done.recv_ref, bf16[624,1024]{1,0:T(8,128)(2,1)} %pad.12.front_h, bf16[1024,1024]{1,0:T(8,128)(2,1)} %expand_h.1, bf16[7,512,256]{2,1,0:T(8,128)(2,1)} %fusion.2.pair_h, bf16[1024,1024]{1,0:T(8,128)(2,1)} %merge_h.1, bf16[1024,128]{1,0:T(8,128)(2,1)S(1)} %copy-done, ...), custom_call_target="tpu_custom_call" | custom-call | flops 20000000000 | bytes 10000000 | tf_op jit(solution)/shard_map/family/pallas_call | solution.py:353
  54.1 8.6 %all-to-all-start.1 = ((bf16[128,4,128]{2,1,0:T(4,128)(2,1)}), bf16[128,4,128]{2,1,0:T(4,128)(2,1)S(1)}, u32[]{:S(2)}, u32[]{:S(2)}) async-start(bf16[128,4,128]{2,1,0:T(4,128)(2,1)} %bitcast.9), calls=%async_computation.1 | async-start | bytes 262144 | tf_op jit(solution)/shard_map/all_to_all | solution.py:468
  62.7 9.7 %all-to-all-done.1 = bf16[128,4,128]{2,1,0:T(4,128)(2,1)S(1)} async-done(((bf16[128,4,128]{2,1,0:T(4,128)(2,1)}), bf16[128,4,128]{2,1,0:T(4,128)(2,1)S(1)}, u32[]{:S(2)}, u32[]{:S(2)}) %all-to-all-start.1) | async-done | bytes 131104 | tf_op jit(solution)/shard_map/all_to_all | solution.py:468
  72.4 1.0 %home.1 = (f32[1,8,107]{2,1,0:T(8,128)}, f32[1,8,64]{2,1,0:T(8,128)}) custom-call(s32[1]{0:T(128)} %bitcast.mem_ref, bf16[512,128]{1,0:T(8,128)(2,1)S(1)} %bitcast.13), custom_call_target="tpu_custom_call" | custom-call | tf_op jit(solution)/shard_map/home/pallas_call | solution.py:410
Async XLA Ops:
  0.6 9.8 %copy-start.5 = (bf16[1,2048,192]{1,2,0:T(8,128)(2,1)S(1)}, bf16[1,2048,192]{1,2,0:T(8,128)(2,1)}, u32[]{:S(2)}) copy-start(bf16[1,2048,192]{1,2,0:T(8,128)(2,1)} %param.22) | copy-start | bytes 2359300
  0.6 11.1 %copy-start.4 = (bf16[400,1024]{1,0:T(8,128)(2,1)S(1)}, bf16[400,1024]{1,0:T(8,128)(2,1)}, u32[]{:S(2)}) copy-start(bf16[400,1024]{1,0:T(8,128)(2,1)} %param.14) | copy-start | bytes 2457604
  2.8 17.9 %all-to-all-start = ((bf16[16,128,128]{2,1,0:T(8,128)(2,1)}), bf16[16,128,128]{2,1,0:T(8,128)(2,1)S(1)}, u32[]{:S(2)}, u32[]{:S(2)}) async-start(bf16[16,128,128]{2,1,0:T(8,128)(2,1)} %pack.1), calls=%async_computation | async-start | bytes 1048576 | tf_op jit(solution)/shard_map/all_to_all | solution.py:451
  10.4 2.6 %copy-start.6 = (bf16[7,384,128]{2,1,0:T(8,128)(2,1)S(1)}, bf16[7,384,128]{2,1,0:T(8,128)(2,1)}, u32[]{:S(2)}) copy-start(bf16[7,384,128]{2,1,0:T(8,128)(2,1)} %param.16) | copy-start | bytes 2064388
  11.7 9.0 %copy-start = (bf16[1024,128]{1,0:T(8,128)(2,1)S(1)}, bf16[1024,128]{1,0:T(8,128)(2,1)}, u32[]{:S(2)}) copy-start(bf16[1024,128]{1,0:T(8,128)(2,1)} %squeeze_h.1) | copy-start | bytes 786436
  11.7 9.0 %copy-start.1 = (bf16[128,1024]{1,0:T(8,128)(2,1)S(1)}, bf16[128,1024]{1,0:T(8,128)(2,1)}, u32[]{:S(2)}) copy-start(bf16[128,1024]{1,0:T(8,128)(2,1)} %excite_h.1) | copy-start | bytes 786436
  11.7 9.0 %copy-start.2 = (bf16[1,128,1024]{2,1,0:T(8,128)(2,1)S(1)}, bf16[1,128,1024]{2,1,0:T(8,128)(2,1)}, u32[]{:S(2)}) copy-start(bf16[1,128,1024]{2,1,0:T(8,128)(2,1)} %param.21) | copy-start | bytes 786436
  11.7 9.0 %copy-start.3 = (bf16[1,192,107]{2,1,0:T(8,128)(2,1)S(1)}, bf16[1,192,107]{2,1,0:T(8,128)(2,1)}, u32[]{:S(2)}) copy-start(bf16[1,192,107]{2,1,0:T(8,128)(2,1)} %param.23) | copy-start | bytes 123268
  54.1 18.3 %all-to-all-start.1 = ((bf16[128,4,128]{2,1,0:T(4,128)(2,1)}), bf16[128,4,128]{2,1,0:T(4,128)(2,1)S(1)}, u32[]{:S(2)}, u32[]{:S(2)}) async-start(bf16[128,4,128]{2,1,0:T(4,128)(2,1)} %bitcast.9), calls=%async_computation.1 | async-start | bytes 262144 | tf_op jit(solution)/shard_map/all_to_all | solution.py:468

commit v6 on v4

--- a/solution.py
+++ b/solution.py
@@ -311,11 +311,12 @@
         for f0 in range(0, FRAMES, pb):
             rows = attended[f0 : f0 + pb].reshape(pb * SLOTS, ATT)
             energy = dot(rows, score_w[:, cols]).reshape(pb, SLOTS, nb)
-            weight = jnp.exp2(energy).astype(BF16)
+            weight = jnp.exp2(energy)
             z = (get(frames, slice(f0, f0 + pb), blocks) - middle[None]) * scale[None]
+            z = z.astype(F32)
             wz = weight * z
-            parts.append((fours(weight), fours(wz), fours(wz * z)))
-        s0, s1, s2 = (slot_sums(jnp.concatenate(part, axis=0)) for part in zip(*parts))
+            parts.append([jnp.sum(part, axis=0) for part in (weight, wz, wz * z)])
+        s0, s1, s2 = (sum(part) for part in zip(*parts))
         m1 = s1 / s0
         m2 = jnp.maximum(s2 / s0 - m1 * m1, 0.0)
         dev = 1.0 / scale.astype(F32)

time: 72.3 us -> 73.2 us (1.012)
  Pallas kernels: 35 us -> 35.9 us
    pallas_call x1, Pallas kernels: 31.8 us -> 32.7 us  [family(): pl.pallas_call(family_kernel, out_shape=jax.ShapeDtypeStruct((SLOTS * 8 *...]
  transfers between devices with their start and end apart: 2 -> 2, of which waited for: 2 -> 2; matrix products, arithmetic and copies ran while one was open for 6% -> 5% of each run, Pallas kernels for 0% -> 0%
where the time goes in v6:
time: 73.2 us; the launch traced here: 72.9 us
  Pallas kernels  35.9 us (49%)
  starting transfers between devices  16.2 us (22%)
  waiting for transfers between devices  16 us (22%)
  local copies, waits for them, and re-layouts  2.55 us (3%)
  other arithmetic  1.47 us (2%)
    pallas_call x1, Pallas kernels, family(): pl.pallas_call(family_kernel, out_shape=jax.ShapeDtypeStruct((SLOTS * 8 *...  32.7 us
    all_to_all x1, waiting for transfers between devices, shards(): lax.all_to_all(scored.reshape(SLOTS * 8, 4, LANES), ('grp', 'mem'), split...  9.75 us
    all_to_all x1, starting transfers between devices, shards(): lax.all_to_all(scored.reshape(SLOTS * 8, 4, LANES), ('grp', 'mem'), split...  8.61 us
    all_to_all x1, starting transfers between devices, shards(): lax.all_to_all(outbound, 'grp', split_axis=0, concat_axis=0, tiled=True)  7.58 us
    all_to_all x1, waiting for transfers between devices, shards(): lax.all_to_all(outbound, 'grp', split_axis=0, concat_axis=0, tiled=True)  6.26 us
    pallas_call x1, Pallas kernels, pack(): pl.pallas_call(pack_kernel, out_shape=jax.ShapeDtypeStruct((SLOTS, ROWS,...  2.15 us
    concatenate x1, other arithmetic, prepare(): return (tall, jnp.concatenate([early, late], axis=2))  1.47 us
  transfers between devices with their start and end apart: 2, of which 2 were waited for; matrix products, arithmetic and copies ran while one was open for 5% of the time, Pallas kernels for 0%

profile of v6, /device:TPU:1, one launch (start us, length us, event | category | flops | bytes accessed | tf_op | source)
XLA Modules:
  0.0 72.9 jit_solution(15296751238874249897)
XLA Ops:
  0.6 0.0 copy-start.5
  0.6 0.0 copy-start.4
  0.7 2.1 %pack.1 = bf16[16,128,128]{2,1,0:T(8,128)(2,1)} custom-call(s32[8]{0:T(128)} %bitcast.18, f32[1000,128]{1,0:T(8,128)} %bitcast.17), custom_call_target="tpu_custom_call" | custom-call | tf_op jit(solution)/shard_map/pack/pallas_call | solution.py:64
  2.8 7.6 %all-to-all-start = ((bf16[16,128,128]{2,1,0:T(8,128)(2,1)}), bf16[16,128,128]{2,1,0:T(8,128)(2,1)S(1)}, u32[]{:S(2)}, u32[]{:S(2)}) async-start(bf16[16,128,128]{2,1,0:T(8,128)(2,1)} %pack.1), calls=%async_computation | async-start | bytes 1048576 | tf_op jit(solution)/shard_map/all_to_all | solution.py:445
  10.4 0.0 copy-done.5
  10.4 0.0 copy-start.6
  10.4 1.3 %copy.14 = bf16[1,2048,192]{2,1,0:T(8,128)(2,1)} copy(bf16[1,2048,192]{1,2,0:T(8,128)(2,1)S(1)} %copy-done.5) | data formatting | bytes 1572864 | tf_op args[10]
  11.7 0.0 copy-done.4
  11.7 0.0 copy-start
  11.7 0.0 copy-start.1
  11.7 0.0 copy-start.2
  11.7 0.0 copy-start.3
  11.7 1.2 %pad.12.front_h = bf16[624,1024]{1,0:T(8,128)(2,1)} pad(bf16[400,1024]{1,0:T(8,128)(2,1)S(1)} %copy-done.4, bf16[]{:T(256)} %constant.6.clone.1), padding=112_112x0_0 | pad | bytes 2097154 | tf_op jit(solution)/shard_map/jit(_pad)/pad | solution.py:422
  13.0 0.0 copy-done.6
  13.0 1.5 %fusion.2.pair_h = bf16[7,512,256]{2,1,0:T(8,128)(2,1)} fusion(bf16[7,384,128]{2,1,0:T(8,128)(2,1)S(1)} %copy-done.6), kind=kLoop, calls=%fused_computation.4 | loop fusion | flops 7340032 | bytes 2523136 | tf_op jit(solution)/shard_map/concatenate | solution.py:425
  14.4 6.3 %all-to-all-done.recv_ref = bf16[16,128,128]{2,1,0:T(8,128)(2,1)S(1)} async-done(((bf16[16,128,128]{2,1,0:T(8,128)(2,1)}), bf16[16,128,128]{2,1,0:T(8,128)(2,1)S(1)}, u32[]{:S(2)}, u32[]{:S(2)}) %all-to-all-start) | async-done | bytes 524320 | tf_op jit(solution)/shard_map/all_to_all | solution.py:445
  20.7 0.0 copy-done
  20.7 0.0 copy-done.1
  20.7 0.0 copy-done.2
  20.7 0.0 copy-done.3
  20.7 32.7 %family.1 = bf16[512,128]{1,0:T(8,128)(2,1)} custom-call(bf16[16,128,128]{2,1,0:T(8,128)(2,1)S(1)} %all-to-all-done.recv_ref, bf16[624,1024]{1,0:T(8,128)(2,1)} %pad.12.front_h, bf16[1024,1024]{1,0:T(8,128)(2,1)} %expand_h.1, bf16[7,512,256]{2,1,0:T(8,128)(2,1)} %fusion.2.pair_h, bf16[1024,1024]{1,0:T(8,128)(2,1)} %merge_h.1, bf16[1024,128]{1,0:T(8,128)(2,1)S(1)} %copy-done, ...), custom_call_target="tpu_custom_call" | custom-call | flops 20000000000 | bytes 10000000 | tf_op jit(solution)/shard_map/family/pallas_call | solution.py:347
  53.5 8.6 %all-to-all-start.1 = ((bf16[128,4,128]{2,1,0:T(4,128)(2,1)}), bf16[128,4,128]{2,1,0:T(4,128)(2,1)S(1)}, u32[]{:S(2)}, u32[]{:S(2)}) async-start(bf16[128,4,128]{2,1,0:T(4,128)(2,1)} %bitcast.9), calls=%async_computation.1 | async-start | bytes 262144 | tf_op jit(solution)/shard_map/all_to_all | solution.py:462
  62.1 9.7 %all-to-all-done.1 = bf16[128,4,128]{2,1,0:T(4,128)(2,1)S(1)} async-done(((bf16[128,4,128]{2,1,0:T(4,128)(2,1)}), bf16[128,4,128]{2,1,0:T(4,128)(2,1)S(1)}, u32[]{:S(2)}, u32[]{:S(2)}) %all-to-all-start.1) | async-done | bytes 131104 | tf_op jit(solution)/shard_map/all_to_all | solution.py:462
  71.8 1.0 %home.1 = (f32[1,8,107]{2,1,0:T(8,128)}, f32[1,8,64]{2,1,0:T(8,128)}) custom-call(s32[1]{0:T(128)} %bitcast.mem_ref, bf16[512,128]{1,0:T(8,128)(2,1)S(1)} %bitcast.13), custom_call_target="tpu_custom_call" | custom-call | tf_op jit(solution)/shard_map/home/pallas_call | solution.py:404
Async XLA Ops:
  0.6 9.8 %copy-start.5 = (bf16[1,2048,192]{1,2,0:T(8,128)(2,1)S(1)}, bf16[1,2048,192]{1,2,0:T(8,128)(2,1)}, u32[]{:S(2)}) copy-start(bf16[1,2048,192]{1,2,0:T(8,128)(2,1)} %param.22) | copy-start | bytes 2359300
  0.6 11.1 %copy-start.4 = (bf16[400,1024]{1,0:T(8,128)(2,1)S(1)}, bf16[400,1024]{1,0:T(8,128)(2,1)}, u32[]{:S(2)}) copy-start(bf16[400,1024]{1,0:T(8,128)(2,1)} %param.14) | copy-start | bytes 2457604
  2.8 17.9 %all-to-all-start = ((bf16[16,128,128]{2,1,0:T(8,128)(2,1)}), bf16[16,128,128]{2,1,0:T(8,128)(2,1)S(1)}, u32[]{:S(2)}, u32[]{:S(2)}) async-start(bf16[16,128,128]{2,1,0:T(8,128)(2,1)} %pack.1), calls=%async_computation | async-start | bytes 1048576 | tf_op jit(solution)/shard_map/all_to_all | solution.py:445
  10.4 2.6 %copy-start.6 = (bf16[7,384,128]{2,1,0:T(8,128)(2,1)S(1)}, bf16[7,384,128]{2,1,0:T(8,128)(2,1)}, u32[]{:S(2)}) copy-start(bf16[7,384,128]{2,1,0:T(8,128)(2,1)} %param.16) | copy-start | bytes 2064388
  11.7 9.0 %copy-start = (bf16[1024,128]{1,0:T(8,128)(2,1)S(1)}, bf16[1024,128]{1,0:T(8,128)(2,1)}, u32[]{:S(2)}) copy-start(bf16[1024,128]{1,0:T(8,128)(2,1)} %squeeze_h.1) | copy-start | bytes 786436
  11.7 9.0 %copy-start.1 = (bf16[128,1024]{1,0:T(8,128)(2,1)S(1)}, bf16[128,1024]{1,0:T(8,128)(2,1)}, u32[]{:S(2)}) copy-start(bf16[128,1024]{1,0:T(8,128)(2,1)} %excite_h.1) | copy-start | bytes 786436
  11.7 9.0 %copy-start.2 = (bf16[1,128,1024]{2,1,0:T(8,128)(2,1)S(1)}, bf16[1,128,1024]{2,1,0:T(8,128)(2,1)}, u32[]{:S(2)}) copy-start(bf16[1,128,1024]{2,1,0:T(8,128)(2,1)} %param.21) | copy-start | bytes 786436
  11.7 9.0 %copy-start.3 = (bf16[1,192,107]{2,1,0:T(8,128)(2,1)S(1)}, bf16[1,192,107]{2,1,0:T(8,128)(2,1)}, u32[]{:S(2)}) copy-start(bf16[1,192,107]{2,1,0:T(8,128)(2,1)} %param.23) | copy-start | bytes 123268
  53.5 18.4 %all-to-all-start.1 = ((bf16[128,4,128]{2,1,0:T(4,128)(2,1)}), bf16[128,4,128]{2,1,0:T(4,128)(2,1)S(1)}, u32[]{:S(2)}, u32[]{:S(2)}) async-start(bf16[128,4,128]{2,1,0:T(4,128)(2,1)} %bitcast.9), calls=%async_computation.1 | async-start | bytes 262144 | tf_op jit(solution)/shard_map/all_to_all | solution.py:462
